TPU v7x, 128 devices: a whole 4x4x4 slice. The times are simulated.
128 devices in a mesh: recv: 32 (over y, x_lo, z), depth: 4 (over x_hi, core).
Axes of the slice: x: 4 (x_hi: 2, x_lo: 2; x = x_hi * 2 + x_lo), y: 4, z: 4, core: 2. Of those that a mesh axis runs over, the one named last changes fastest.
Arguments:
- displace: bfloat16 [4, 32, 2, 8, 32, 128], P(None, 'recv', None, None, 'depth'), may hold values from -6 to 6
- green: bfloat16 [128, 2, 2, 8, 32, 128], P('recv', None, None, None, 'depth'), may hold values from -6 to 6
- pair_src: int32 [4, 128], P(None, 'recv'), may hold values from 0 to 31
- source_at: int32 [4, 32], replicated, may hold values from 0 to 31, each once within a row
Outputs:
- kernels: bfloat16 [4, 128, 2, 2, 9, 32, 128], P(None, 'recv', None, None, None, 'depth')
Inputs may be any that keep to these rules, and one draw needn't show every extreme that they name: `source_at`: each row is a permutation of the slots.
All inputs are finite; a program needn't handle non-finite values.
Results may differ from a plain program's by a relative error of at most 0.0058.
Values may be sent and summed in bfloat16 or wider, within the bound.
No kernel may reach another device: no remote copies, remote signals or barrier semaphores. Data moves between devices by JAX's collectives and lax.ppermute only.
A program may use at most 128 MiB of HBM per device.

v0:
```python
import jax
import jax.numpy as jnp
from jax import lax
from jax.sharding import PartitionSpec as P

LAGS = 9


def padded_2(block, sides, width):
    for axis, dim in sides:
        count = lax.axis_size(axis)
        forward = [(i, i + 1) for i in range(count - 1)]
        backward = [(target, source) for source, target in forward]
        low = lax.ppermute(
            lax.slice_in_dim(block, block.shape[dim] - width, None, axis=dim), axis, forward
        )
        high = lax.ppermute(lax.slice_in_dim(block, 0, width, axis=dim), axis, backward)
        block = jnp.concatenate([low, block, high], axis=dim)
    return block


def strain_of(padded, heights):

    def ddx(v):
        return (jnp.roll(v, -1, -1) - jnp.roll(v, 1, -1)) * 0.5

    def ddz(v):
        return (v[..., 2:, :] - v[..., :-2, :]) / (2.0 * heights[:, None])

    wx = padded[..., 0, :, :, :]
    wz = padded[..., 1, :, :, :]
    exx = ddx(wx[..., 1:-1, :])
    ezz = ddz(wz)
    exz = 0.5 * (ddz(wx) + ddx(wz[..., 1:-1, :]))
    return jnp.stack([exx, ezz, exz], axis=-4).astype(jnp.bfloat16)


def kernels_of(source_part, green_part):
    steps = source_part.shape[-3]
    div_source = source_part[..., 0, :, :, :] + source_part[..., 1, :, :, :]
    div_green = green_part[..., 0, :, :, :] + green_part[..., 1, :, :, :]
    weights = jnp.array([2.0, 2.0, 4.0], dtype=jnp.float32)[:, None, None, None]
    weighted = source_part * weights
    lam_list = []
    shear_list = []
    for lag in range(LAGS):
        offset = lag - LAGS // 2
        first = max(0, -offset)
        last = min(steps, steps - offset)
        lam_list.append(
            jnp.sum(
                div_source[..., first:last, :, :]
                * div_green[..., first + offset : last + offset, :, :],
                axis=-3,
            )
        )
        shear_list.append(
            jnp.sum(
                weighted[..., first:last, :, :]
                * green_part[..., first + offset : last + offset, :, :],
                axis=(-4, -3),
            )
        )
    lam = jnp.stack(lam_list, axis=-3)
    shear = jnp.stack(shear_list, axis=-3)
    return jnp.stack([lam, shear], axis=-5)


def picker(round_slots, piece):
    count = piece.shape[1]
    columns = jnp.arange(count, dtype=jnp.int32)
    onehot = (round_slots[:, :, None] == columns[None, None, :]).astype(jnp.bfloat16)
    return jnp.einsum("krj,kjm->krm", onehot, piece, preferred_element_type=jnp.float32)


def shards(displace, green, pair_src, source_at):
    rounds = displace.shape[0]
    rows_dev = displace.shape[4]
    receivers = green.shape[0]
    nsrc = source_at.shape[1]
    depth_total = rows_dev * lax.axis_size("depth")
    rows = lax.axis_index("depth") * rows_dev + jnp.arange(rows_dev, dtype=jnp.int32)
    heights = 0.5 + 1.5 * (rows.astype(jnp.float32) + 0.5) / depth_total
    match = pair_src[:, :, None] == jnp.arange(nsrc, dtype=jnp.int32)[None, None, :]
    slots = jnp.sum(jnp.where(match, source_at[:, None, :], 0), axis=2)
    green_pad = padded_2(green, (("depth", 4),), 1)
    green_strain = strain_of(green_pad.astype(jnp.float32), heights)
    comps = displace.shape[2]
    flat = displace.reshape(rounds, displace.shape[1], -1)
    collected = []
    for round_id in range(rounds):
        collected.append(
            picker(
                slots[round_id : round_id + 1],
                lax.all_gather(flat[round_id : round_id + 1], "recv", axis=1, tiled=True),
            )
        )
    picked = jnp.concatenate(collected, axis=0)
    picked = picked.astype(jnp.bfloat16).reshape(
        rounds, receivers, comps, displace.shape[3], rows_dev, displace.shape[5]
    )
    padded = padded_2(picked, (("depth", 4),), 1)
    source_strain = strain_of(padded.astype(jnp.float32), heights)
    result = kernels_of(
        source_strain.astype(jnp.float32)[:, :, None], green_strain.astype(jnp.float32)[None]
    )
    return result.astype(jnp.bfloat16)


def solution(mesh):
    return jax.shard_map(
        shards,
        mesh=mesh,
        in_specs=(
            P(None, "recv", None, None, "depth", None),
            P("recv", None, None, None, "depth", None),
            P(None, "recv"),
            P(),
        ),
        out_specs=P(None, "recv", None, None, None, "depth", None),
        check_vma=False,
    )
```

profile of v0, /device:TPU:4, one launch (start us, length us, event | category | flops | bytes accessed | tf_op | source)
XLA Modules:
  0.0 658.3 jit_solution(12815716857645784505)
XLA Ops:
  12.7 2.4 collective-permute-start.2
  16.7 7.2 %copy.234 = bf16[4,2,2,8,8,128]{4,3,1,0,5,2:T(8,128)(2,1)} copy(bf16[4,2,2,8,8,128]{5,4,3,2,1,0:T(8,128)(2,1)} %param.6) | data formatting | bytes 524288 | tf_op args[1]
  23.9 6.8 %copy.235 = bf16[4,2,2,8,1,128]{4,3,1,0,5,2:T(8,128)(2,1)} copy(bf16[4,2,2,8,1,128]{5,3,4,2,1,0:T(8,128)(2,1)S(1)} %collective-permute-done.3) | data formatting | bytes 65536 | tf_op jit(solution)/shard_map/ppermute | solution.py:17
  30.7 6.8 %copy.233 = bf16[4,2,2,8,1,128]{4,3,1,0,5,2:T(8,128)(2,1)} copy(bf16[4,2,2,8,1,128]{5,3,4,2,1,0:T(8,128)(2,1)S(1)} %collective-permute-done.2) | data formatting | bytes 65536 | tf_op jit(solution)/shard_map/ppermute | solution.py:14
  37.5 6.5 maximum_convert_fusion
  45.7 2.2 fusion.46
  48.1 5.4 slice_bitcast_fusion.2
  53.5 4.7 fusion.4
  58.1 3.2 copy.242
  61.3 2.1 copy.241
  63.9 3.8 copy.236
  67.7 3.8 copy.239
  75.3 3.8 copy.250
  79.1 2.8 copy.249
  84.9 78.8 %all-gather.11.cloned.1.call-done = bf16[1,32,16384]{2,0,1:T(2,128)(2,1)} async-done(((bf16[1,1,16384]{2,0,1:T(2,128)(2,1)}), bf16[1,32,16384]{2,0,1:T(2,128)(2,1)}) %all-gather.11.cloned.1.call-update) | async-done | bytes 1048592 | tf_op jit(solution)/shard_map/all_gather | solution.py:95
  163.7 2.7 copy.310
  167.4 150.6 %all-gather.9.cloned.1.call-done = bf16[1,32,16384]{2,0,1:T(2,128)(2,1)} async-done(((bf16[1,1,16384]{2,0,1:T(2,128)(2,1)}), bf16[1,32,16384]{2,0,1:T(2,128)(2,1)}) %all-gather.9.cloned.1.call-update) | async-done | bytes 1048592 | tf_op jit(solution)/shard_map/all_gather | solution.py:95
  318.1 2.7 copy.311
  321.7 150.6 %all-gather.7.cloned.1.call-done = bf16[1,32,16384]{2,0,1:T(2,128)(2,1)} async-done(((bf16[1,1,16384]{2,0,1:T(2,128)(2,1)}), bf16[1,32,16384]{2,0,1:T(2,128)(2,1)}) %all-gather.7.cloned.1.call-update) | async-done | bytes 1048592 | tf_op jit(solution)/shard_map/all_gather | solution.py:95
  472.4 2.7 copy.312
  476.1 150.5 %all-gather.5.cloned.1.call-done = bf16[1,32,16384]{2,0,1:T(2,128)(2,1)} async-done(((bf16[1,1,16384]{2,0,1:T(2,128)(2,1)}), bf16[1,32,16384]{2,0,1:T(2,128)(2,1)}) %all-gather.5.cloned.1.call-update) | async-done | bytes 1048592 | tf_op jit(solution)/shard_map/all_gather | solution.py:95
  626.6 2.7 copy.313
  632.4 2.6 collective-permute-start
  635.2 5.1 collective-permute-done
  (140 shorter events, 33.4 us)
Async XLA Ops:
  6.5 157.2 %all-gather.11.cloned.1.call-start = ((), (), s32[]{:S(2)}) async-start(), calls=%async_computation.3 | async-start | bytes 2162688 | tf_op jit(solution)/shard_map/all_gather | solution.py:95
  8.0 310.0 %all-gather.9.cloned.1.call-start = ((), (), s32[]{:S(2)}) async-start(), calls=%async_computation.2 | async-start | bytes 2162688 | tf_op jit(solution)/shard_map/all_gather | solution.py:95
  8.8 463.6 %all-gather.7.cloned.1.call-start = ((), (), s32[]{:S(2)}) async-start(), calls=%async_computation.1 | async-start | bytes 2162688 | tf_op jit(solution)/shard_map/all_gather | solution.py:95
  9.5 617.0 %all-gather.5.cloned.1.call-start = ((), (), s32[]{:S(2)}) async-start(), calls=%async_computation | async-start | bytes 2162688 | tf_op jit(solution)/shard_map/all_gather | solution.py:95
  10.7 13.2 %collective-permute-start.3 = (bf16[4,2,2,8,1,128]{5,3,4,2,1,0:T(8,128)(2,1)S(1)}, bf16[4,2,2,8,1,128]{5,3,4,2,1,0:T(8,128)(2,1)S(1)}, u32[]{:S(2)}, u32[]{:S(2)}) collective-permute-start(bf16[4,2,2,8,1,128]{5,3,4,2,1,0:T(8,128)(2,1)S(1)} %copy.265), channel_id=1, source_target_pairs={{1,0},{2,1},{3,2},{5,4},{6,5},{7,6},{9,8},{10,9},{11,10},{13,12},{... | collective-permute-start | bytes 98312 | tf_op jit(solution)/shard_map/ppermute | solution.py:17
  12.7 18.1 %collective-permute-start.2 = (bf16[4,2,2,8,1,128]{5,3,4,2,1,0:T(8,128)(2,1)S(1)}, bf16[4,2,2,8,1,128]{5,3,4,2,1,0:T(8,128)(2,1)S(1)}, u32[]{:S(2)}, u32[]{:S(2)}) collective-permute-start(bf16[4,2,2,8,1,128]{5,3,4,2,1,0:T(8,128)(2,1)S(1)} %copy.264), channel_id=1, source_target_pairs={{0,1},{1,2},{2,3},{4,5},{5,6},{6,7},{8,9},{9,10},{10,11},{12,13},{... | collective-permute-start | bytes 98312 | tf_op jit(solution)/shard_map/ppermute | solution.py:14
  72.2 3.2 copy-start.4
  629.3 5.8 copy-start.5
  629.3 5.8 copy-start.13
  629.3 5.8 copy-start.14
  630.5 4.7 collective-permute-start.1
  632.4 7.8 %collective-permute-start = (bf16[4,4,2,8,1,128]{5,4,3,1,0,2:T(2,128)(2,1)S(1)}, bf16[4,4,2,8,1,128]{5,4,3,1,0,2:T(2,128)(2,1)S(1)}, u32[]{:S(2)}, u32[]{:S(2)}) collective-permute-start(bf16[4,4,2,8,1,128]{5,4,3,1,0,2:T(2,128)(2,1)S(1)} %get-tuple-element.53), channel_id=1, source_target_pairs={{0,1},{1,2},{2,3},{4,5},{5,6},{6,7},{8,9},{9,10},{10,11},{12,13},{... | collective-permute-start | bytes 196616 | tf_op jit(solution)/shard_map/ppermute | solution.py:14
  644.3 1.0 copy-start.2
  644.3 1.1 copy-start.3
  644.4 1.4 copy-start.15
  644.4 1.4 copy-start.16
  644.5 1.5 copy-start
  644.5 1.5 copy-start.1
  648.0 1.0 copy-start.12
  648.0 1.1 copy-start.9
  648.0 1.2 copy-start.10
  648.3 1.1 copy-start.7
  648.3 1.1 copy-start.8
  649.0 1.0 copy-start.6
  (2 other events, 1.6 us)
Sparse Core Ops, SparseCore 0:
  9.0 154.7 all-gather.10
  165.4 152.6 all-gather.8
  319.7 152.6 all-gather.6
  473.9 152.6 all-gather.4
where the time goes:
time: 667 us; the launch traced here: 658 us
  waiting for transfers between devices  536 us (80%)
  local copies, waits for them, and re-layouts  78 us (12%)
  other arithmetic  18.7 us (3%)
  between operations  14.1 us (2%)
  starting transfers between devices  8.99 us (1%)
    all_gather x4, waiting for transfers between devices, shards(): lax.all_gather(flat[round_id:round_id + 1], 'recv', axis=1, tiled=True)  531 us
    unnamed x63, local copies, waits for them, and re-layouts  21.6 us
    concatenate x8, local copies, waits for them, and re-layouts, ddx(): return (jnp.roll(v, -1, -1) - jnp.roll(v, 1, -1)) * 0.5  14.5 us
  transfers between devices with their start and end apart: 8, of which 5 were waited for; matrix products, arithmetic and copies ran while one was open for 13% of the time, Pallas kernels for 0%

commit v1 on v0

v1 whole, which is shorter than its diff:
```python
import jax
import jax.numpy as jnp
from jax import lax
from jax.experimental import pallas as pl
from jax.experimental.pallas import tpu as pltpu
from jax.sharding import PartitionSpec as P

LAGS = 9
F32 = jnp.float32
BF16 = jnp.bfloat16
VMEM = pl.BlockSpec(memory_space=pltpu.VMEM)
SMEM = pl.BlockSpec(memory_space=pltpu.SMEM)


def inverse_spacing():
    depth = lax.axis_index("depth")
    total = 8 * lax.axis_size("depth")
    row = (lax.broadcasted_iota(jnp.int32, (8, 128), 0) + depth * 8).astype(F32)
    heights = 0.5 + 1.5 * (row + 0.5) / total
    return 1.0 / (2.0 * heights)


def strain_of(wx, wz, lo_x, hi_x, lo_z, hi_z, inverse, row):
    def ddx(v):
        return (pltpu.roll(v, 127, 1) - pltpu.roll(v, 1, 1)) * 0.5

    def ddz(v, lo, hi):
        after = jnp.where(row == 7, hi, pltpu.roll(v, 7, 0))
        before = jnp.where(row == 0, lo, pltpu.roll(v, 1, 0))
        return (after - before) * inverse

    return ddx(wx), ddz(wz, lo_z, hi_z), 0.5 * (ddz(wx, lo_x, hi_x) + ddx(wz))


def edges_kernel(displace_ref, green_ref, first_ref, second_ref):
    odd = lax.rem(lax.axis_index("depth"), 2) == 1
    base = 0
    for ref in (displace_ref, green_ref):
        for start in range(0, ref.shape[0], 16):
            slabs = ref[start : start + 16].astype(F32)
            top, bottom = slabs[:, 0, :], slabs[:, 7, :]
            first_ref[base + start : base + start + 16] = jnp.where(odd, top, bottom).astype(BF16)
            second_ref[base + start : base + start + 16] = jnp.where(odd, bottom, top).astype(BF16)
        base += ref.shape[0]


def pack_kernel(pair_ref, at_ref, displace_ref, first_ref, second_ref, out_ref):
    rounds, comps, steps = displace_ref.shape[:3]
    odd = lax.rem(lax.axis_index("depth"), 2) == 1
    row = lax.broadcasted_iota(jnp.int32, (8, 128), 0)
    lane = lax.broadcasted_iota(jnp.int32, (8, 128), 1)
    for k in range(rounds):
        extra = jnp.zeros((8, 128), F32)
        for r in range(pair_ref.shape[1]):
            slot = at_ref[k, pair_ref[k, r]].astype(F32)
            extra = jnp.where((row == 4) & (lane == r), slot, extra)
        halos = []
        for c in range(comps):
            at = (k * comps + c) * steps
            one = first_ref[at : at + steps].astype(F32)
            two = second_ref[at : at + steps].astype(F32)
            halos += [jnp.where(odd, one, two), jnp.where(odd, two, one)]
        for t in range(steps):
            p = k * steps + t
            for c in range(comps):
                out_ref[p, c] = displace_ref[k, c, t]
            tile = extra
            for i, halo in enumerate(halos):
                tile = jnp.where(row == i, jnp.broadcast_to(halo[t : t + 1], (8, 128)), tile)
            out_ref[p, 2] = tile.astype(BF16)


def select_kernel(in_ref, out_ref, strain_ref, slots_ref, scalars_ref, sem):
    sources, receivers = in_ref.shape[0], out_ref.shape[1] // 3
    inverse = inverse_spacing()
    row = lax.broadcasted_iota(jnp.int32, (8, 128), 0)
    for s in range(sources):
        slots_ref[s : s + 1] = in_ref[s, 2].astype(F32)[4:5].astype(jnp.int32)
    copy = pltpu.make_async_copy(slots_ref, scalars_ref, sem)
    copy.start()

    def strain_step(s, carry):
        tile = in_ref[s, 2].astype(F32)
        lo_x, hi_x, lo_z, hi_z = (jnp.broadcast_to(tile[i : i + 1], (8, 128)) for i in range(4))
        wx, wz = in_ref[s, 0].astype(F32), in_ref[s, 1].astype(F32)
        for c, part in enumerate(strain_of(wx, wz, lo_x, hi_x, lo_z, hi_z, inverse, row)):
            strain_ref[s, c] = part.astype(BF16)
        return carry

    lax.fori_loop(0, sources, strain_step, 0, unroll=4)
    copy.wait()

    def select_step(d, carry):
        for r in range(receivers):
            s = scalars_ref[d, r]
            for c in range(3):
                out_ref[d, r * 3 + c] = strain_ref[s, c]
        return carry

    lax.fori_loop(0, sources, select_step, 0, unroll=4)


def correlate_kernel(source_ref, green_ref, first_ref, second_ref, out_ref, green_strain_ref):
    forces, comps, steps = green_ref.shape[1:4]

    @pl.when(pl.program_id(1) == 0)
    def _():
        odd = lax.rem(lax.axis_index("depth"), 2) == 1
        inverse = inverse_spacing()
        row = lax.broadcasted_iota(jnp.int32, (8, 128), 0)
        for f in range(forces):
            halos = []
            for c in range(comps):
                at = (f * comps + c) * steps
                one = first_ref[0, at : at + steps].astype(F32)
                two = second_ref[0, at : at + steps].astype(F32)
                halos += [jnp.where(odd, one, two), jnp.where(odd, two, one)]
            for t in range(steps):
                rows = [jnp.broadcast_to(halo[t : t + 1], (8, 128)) for halo in halos]
                wx, wz = green_ref[0, f, 0, t].astype(F32), green_ref[0, f, 1, t].astype(F32)
                b0, b1, b2 = (b.astype(BF16).astype(F32) for b in strain_of(wx, wz, *rows, inverse, row))
                green_strain_ref[f, t, 0] = b0 + b1
                green_strain_ref[f, t, 1] = b0 - b1
                green_strain_ref[f, t, 2] = b2

    total, spread, cross = [], [], []
    for t in range(steps):
        a0, a1, a2 = (source_ref[t, c].astype(F32) for c in range(3))
        total.append(a0 + a1)
        spread.append(a0 - a1)
        cross.append(a2 * 4.0)
    for f in range(forces):
        for lag in range(LAGS):
            offset = lag - LAGS // 2
            lam = shear = None
            for t in range(max(0, -offset), min(steps, steps - offset)):
                u = t + offset
                x = total[t] * green_strain_ref[f, u, 0]
                y = spread[t] * green_strain_ref[f, u, 1] + cross[t] * green_strain_ref[f, u, 2]
                lam = x if lam is None else lam + x
                shear = y if shear is None else shear + y
            out_ref[0, 0, 0, f, lag] = lam.astype(BF16)
            out_ref[0, 0, 1, f, lag] = (lam + shear).astype(BF16)


def shards(displace, green, pair_src, source_at):
    rounds, _, comps, steps, rows, cells = displace.shape
    receivers, forces = green.shape[:2]
    sources = source_at.shape[1]
    assert rounds * steps == lax.axis_size("recv") == sources
    assert (rows, cells, lax.axis_size("depth")) == (8, 128, 4)

    own = rounds * comps * steps
    far = receivers * forces * comps * steps
    edges = jax.ShapeDtypeStruct((own + far, cells), BF16)
    first, second = pl.pallas_call(
        edges_kernel, out_shape=(edges, edges), in_specs=[VMEM] * 2, out_specs=(VMEM, VMEM), name="edges"
    )(displace.reshape(own, rows, cells), green.reshape(far, rows, cells))
    second = lax.ppermute(second, "depth", [(1, 2), (2, 1)])
    first = lax.ppermute(first, "depth", [(0, 1), (1, 0), (2, 3), (3, 2)])

    packed = pl.pallas_call(
        pack_kernel,
        out_shape=jax.ShapeDtypeStruct((sources, 3, rows, cells), BF16),
        in_specs=[SMEM, SMEM, VMEM, VMEM, VMEM],
        out_specs=VMEM,
        name="pack",
    )(pair_src, source_at, displace.reshape(rounds, comps, steps, rows, cells), first, second)
    pieces = lax.all_to_all(packed, "recv", 0, 0, tiled=True)
    chosen = pl.pallas_call(
        select_kernel,
        out_shape=jax.ShapeDtypeStruct((sources, receivers * 3, rows, cells), BF16),
        in_specs=[VMEM],
        out_specs=VMEM,
        scratch_shapes=[
            pltpu.VMEM((sources, 3, rows, cells), BF16),
            pltpu.VMEM((sources, cells), jnp.int32),
            pltpu.SMEM((sources, cells), jnp.int32),
            pltpu.SemaphoreType.DMA,
        ],
        name="select",
    )(pieces)
    paired = lax.all_to_all(chosen, "recv", 0, 0, tiled=True)
    per = forces * comps * steps
    skip = own // per
    halo = pl.BlockSpec((1, per, cells), lambda r, k: (r + skip, 0, 0))
    return pl.pallas_call(
        correlate_kernel,
        grid=(receivers, rounds),
        out_shape=jax.ShapeDtypeStruct((rounds, receivers, 2, forces, LAGS, rows, cells), BF16),
        in_specs=[
            pl.BlockSpec((steps, 3, rows, cells), lambda r, k: (k, r, 0, 0)),
            pl.BlockSpec((1, forces, comps, steps, rows, cells), lambda r, k: (r, 0, 0, 0, 0, 0)),
            halo,
            halo,
        ],
        out_specs=pl.BlockSpec((1, 1, 2, forces, LAGS, rows, cells), lambda r, k: (k, r, 0, 0, 0, 0, 0)),
        scratch_shapes=[pltpu.VMEM((forces, steps, 3, rows, cells), F32)],
        name="correlate",
    )(paired, green, first.reshape(-1, per, cells), second.reshape(-1, per, cells))


def solution(mesh):
    return jax.shard_map(
        shards,
        mesh=mesh,
        in_specs=(
            P(None, "recv", None, None, "depth", None),
            P("recv", None, None, None, "depth", None),
            P(None, "recv"),
            P(),
        ),
        out_specs=P(None, "recv", None, None, None, "depth", None),
        check_vma=False,
    )
```

time: 667 us -> 58.6 us (0.09); the launches traced: 658 us -> 57.6 us
  waiting for transfers between devices: 536 us -> 4.68 us
  local copies, waits for them, and re-layouts: 78 us -> 0.62 us
  blocking collectives: 0 us -> 33.8 us
  other arithmetic: 18.7 us -> 0 us
  Pallas kernels: 0 us -> 16.1 us
  between operations: 14.1 us -> 0.04 us
    all_gather x4 -> x0, waiting for transfers between devices: 531 us -> none  [shards(): lax.all_gather(flat[round_id:round_id + 1], 'recv', axis=1, tiled=True)]
    all_to_all x0 -> x2, blocking collectives: none -> 33.8 us  [the longest x1 18 us: shards(): pieces = lax.all_to_all(packed, 'recv', 0, 0, tiled=True)]
    unnamed x63 -> x4, local copies, waits for them, and re-layouts: 21.6 us -> 0.62 us
    pallas_call x0 -> x4, Pallas kernels: none -> 16.1 us  [the longest x1 9.57 us: shards(): pl.pallas_call(correlate_kernel, grid=(receivers, rounds), out_shape=jax....]
    concatenate x8 -> x0, local copies, waits for them, and re-layouts: 14.5 us -> none  [ddx(): return (jnp.roll(v, -1, -1) - jnp.roll(v, 1, -1)) * 0.5]
    ppermute x2 -> x0, local copies, waits for them, and re-layouts: 13.6 us -> none  [the longest x1 6.81 us: padded_2(): lax.ppermute(lax.slice_in_dim(block, 0, width, axis=dim), axis, backward)]
    another operation x7 -> x0, local copies, waits for them, and re-layouts: 13.1 us -> none  [the longest x4 11.9 us: strain_of(): return jnp.stack([exx, ezz, exz], axis=-4).astype(jnp.bfloat16)]
    convert_element_type x5 -> x0, other arithmetic: 7.31 us -> none  [the longest x1 6.49 us: shards(): green_strain = strain_of(green_pad.astype(jnp.float32), heights)]
  transfers between devices with their start and end apart: 8 -> 2, of which waited for: 5 -> 1; matrix products, arithmetic and copies ran while one was open for 13% -> 0% of each run, Pallas kernels for 0% -> 0%
where the time goes in v1:
time: 58.6 us; the launch traced here: 57.6 us
  blocking collectives  33.8 us (58%)
  Pallas kernels  16.1 us (27%)
  waiting for transfers between devices  4.68 us (8%)
  starting transfers between devices  2.41 us (4%)
  local copies, waits for them, and re-layouts  0.62 us (1%)
    all_to_all x1, blocking collectives, shards(): pieces = lax.all_to_all(packed, 'recv', 0, 0, tiled=True)  18 us
    all_to_all x1, blocking collectives, shards(): paired = lax.all_to_all(chosen, 'recv', 0, 0, tiled=True)  15.8 us
    pallas_call x1, Pallas kernels, shards(): pl.pallas_call(correlate_kernel, grid=(receivers, rounds), out_shape=jax....  9.57 us
    ppermute x1, waiting for transfers between devices, shards(): second = lax.ppermute(second, 'depth', [(1, 2), (2, 1)])  4.68 us
    pallas_call x1, Pallas kernels, shards(): pl.pallas_call(select_kernel, out_shape=jax.ShapeDtypeStruct((sources, re...  2.83 us
    ppermute x1, starting transfers between devices, shards(): second = lax.ppermute(second, 'depth', [(1, 2), (2, 1)])  2.4 us
    pallas_call x1, Pallas kernels, shards(): pl.pallas_call(edges_kernel, out_shape=(edges, edges), in_specs=[VMEM] *...  1.96 us
    pallas_call x1, Pallas kernels, shards(): pl.pallas_call(pack_kernel, out_shape=jax.ShapeDtypeStruct((sources, 3, r...  1.69 us
  transfers between devices with their start and end apart: 2, of which 1 were waited for; matrix products, arithmetic and copies ran while one was open for 0% of the time, Pallas kernels for 0%

profile of v1, /device:TPU:4, one launch (start us, length us, event | category | flops | bytes accessed | tf_op | source)
XLA Modules:
  0.0 57.6 jit_solution(2415690184844878865)
XLA Ops:
  0.0 2.0 %edges.1 = (bf16[192,128]{1,0:T(8,128)(2,1)}, bf16[192,128]{1,0:T(8,128)(2,1)}) custom-call(bf16[64,8,128]{2,1,0:T(8,128)(2,1)} %bitcast.6, bf16[128,8,128]{2,1,0:T(8,128)(2,1)} %bitcast.5), custom_call_target="tpu_custom_call" | custom-call | tf_op jit(solution)/shard_map/edges/pallas_call | solution.py:156
  2.0 0.0 collective-permute-start
  2.0 2.4 %collective-permute-start.1 = (bf16[192,128]{1,0:T(8,128)(2,1)}, bf16[192,128]{1,0:T(8,128)(2,1)S(1)}, u32[]{:S(2)}, u32[]{:S(2)}) collective-permute-start(bf16[192,128]{1,0:T(8,128)(2,1)} %get-tuple-element.8), channel_id=1, source_target_pairs={{1,2},{2,1},{5,6},{6,5},{9,10},{10,9},{13,14},{14,13},{17,18},{18,... | collective-permute-start | bytes 147464 | tf_op jit(solution)/shard_map/ppermute | solution.py:159
  4.4 0.0 collective-permute-done.first_ref
  4.4 0.0 copy-start
  4.4 4.7 %collective-permute-done.1.second_ref = bf16[192,128]{1,0:T(8,128)(2,1)S(1)} collective-permute-done((bf16[192,128]{1,0:T(8,128)(2,1)}, bf16[192,128]{1,0:T(8,128)(2,1)S(1)}, u32[]{:S(2)}, u32[]{:S(2)}) %collective-permute-start.1) | collective-permute-done | bytes 49184 | tf_op jit(solution)/shard_map/ppermute | solution.py:159
  9.1 0.0 copy-start.1
  9.1 0.0 copy-done
  9.1 0.6 %copy-done.1 = bf16[192,128]{1,0:T(8,128)(2,1)} copy-done((bf16[192,128]{1,0:T(8,128)(2,1)}, bf16[192,128]{1,0:T(8,128)(2,1)S(1)}, u32[]{:S(2)}) %copy-start.1) | copy-done | bytes 49176
  9.7 1.7 %pack.1 = bf16[32,3,8,128]{3,2,1,0:T(8,128)(2,1)} custom-call(s32[4,4]{1,0:T(4,128)} %pair_ref.1, s32[4,32]{1,0:T(4,128)} %at_ref.1, bf16[4,2,8,8,128]{4,3,2,1,0:T(8,128)(2,1)} %bitcast.7, bf16[192,128]{1,0:T(8,128)(2,1)} %copy-done, bf16[192,128]{1,0:T(8,128)(2,1)} %copy-done.1), custom_call_target="tpu_custom_call" | custom-call | tf_op jit(solution)/shard_map/pack/pallas_call | solution.py:162
  11.4 18.0 %all_to_all.10.in_ref = bf16[32,3,8,128]{3,2,1,0:T(8,128)(2,1)} all-to-all(bf16[32,3,8,128]{3,2,1,0:T(8,128)(2,1)} %pack.1), channel_id=1, replica_groups=mesh['recv'=32,'depth'=4] {'recv'}, dimensions={0} | all-to-all | bytes 393216 | tf_op jit(solution)/shard_map/all_to_all | solution.py:169
  29.4 2.8 %select.1 = bf16[32,12,8,128]{3,2,1,0:T(8,128)(2,1)} custom-call(bf16[32,3,8,128]{3,2,1,0:T(8,128)(2,1)} %all_to_all.10.in_ref), custom_call_target="tpu_custom_call" | custom-call | tf_op jit(solution)/shard_map/select/pallas_call | solution.py:170
  32.2 15.8 %all_to_all.11.source_ref = bf16[32,12,8,128]{3,2,1,0:T(8,128)(2,1)} all-to-all(bf16[32,12,8,128]{3,2,1,0:T(8,128)(2,1)} %select.1), channel_id=1, replica_groups=mesh['recv'=32,'depth'=4] {'recv'}, dimensions={0} | all-to-all | bytes 1572864 | tf_op jit(solution)/shard_map/all_to_all | solution.py:183
  48.0 9.6 %correlate.1 = bf16[4,4,2,2,9,8,128]{6,5,4,3,2,1,0:T(8,128)(2,1)} custom-call(bf16[32,12,8,128]{3,2,1,0:T(8,128)(2,1)} %all_to_all.11.source_ref, bf16[4,2,2,8,8,128]{5,4,3,2,1,0:T(8,128)(2,1)} %green_ref.1, bf16[6,32,128]{2,1,0:T(8,128)(2,1)} %bitcast.8, bf16[6,32,128]{2,1,0:T(8,128)(2,1)} %bitcast.9), custom_call_target="tpu_custom_call" | custom-call | tf_op jit(solution)/shard_map/correlate/pallas_call | solution.py:187
Async XLA Ops:
  2.0 2.4 %collective-permute-start = (bf16[192,128]{1,0:T(8,128)(2,1)}, bf16[192,128]{1,0:T(8,128)(2,1)S(1)}, u32[]{:S(2)}, u32[]{:S(2)}) collective-permute-start(bf16[192,128]{1,0:T(8,128)(2,1)} %get-tuple-element.7), channel_id=1, source_target_pairs={{0,1},{1,0},{2,3},{3,2},{4,5},{5,4},{6,7},{7,6},{8,9},{9,8},{10,11... | collective-permute-start | bytes 147464 | tf_op jit(solution)/shard_map/ppermute | solution.py:160
  2.0 7.1 %collective-permute-start.1 = (bf16[192,128]{1,0:T(8,128)(2,1)}, bf16[192,128]{1,0:T(8,128)(2,1)S(1)}, u32[]{:S(2)}, u32[]{:S(2)}) collective-permute-start(bf16[192,128]{1,0:T(8,128)(2,1)} %get-tuple-element.8), channel_id=1, source_target_pairs={{1,2},{2,1},{5,6},{6,5},{9,10},{10,9},{13,14},{14,13},{17,18},{18,... | collective-permute-start | bytes 147464 | tf_op jit(solution)/shard_map/ppermute | solution.py:159
  4.4 4.7 %copy-start = (bf16[192,128]{1,0:T(8,128)(2,1)}, bf16[192,128]{1,0:T(8,128)(2,1)S(1)}, u32[]{:S(2)}) copy-start(bf16[192,128]{1,0:T(8,128)(2,1)S(1)} %collective-permute-done.first_ref) | copy-start | bytes 147460
  9.1 0.6 %copy-start.1 = (bf16[192,128]{1,0:T(8,128)(2,1)}, bf16[192,128]{1,0:T(8,128)(2,1)S(1)}, u32[]{:S(2)}) copy-start(bf16[192,128]{1,0:T(8,128)(2,1)S(1)} %collective-permute-done.1.second_ref) | copy-start | bytes 147460

commit v2 on v1

v2 whole, which is shorter than its diff:
```python
import jax
import jax.numpy as jnp
from jax import lax
from jax.experimental import pallas as pl
from jax.experimental.pallas import tpu as pltpu
from jax.sharding import PartitionSpec as P

LAGS = 9
F32 = jnp.float32
BF16 = jnp.bfloat16
VMEM = pl.BlockSpec(memory_space=pltpu.VMEM)
SMEM = pl.BlockSpec(memory_space=pltpu.SMEM)
ANY = pl.BlockSpec(memory_space=pl.ANY)
SAME_CHIP = [(0, 1), (1, 0), (2, 3), (3, 2)]
NEXT_CHIP = [(1, 2), (2, 1)]


def pinned(*arrays):
    return [pltpu.with_memory_space_constraint(a, pltpu.VMEM) for a in arrays]


def inverse_spacing():
    depth = lax.axis_index("depth")
    total = 8 * lax.axis_size("depth")
    row = (lax.broadcasted_iota(jnp.int32, (8, 128), 0) + depth * 8).astype(F32)
    heights = 0.5 + 1.5 * (row + 0.5) / total
    return 1.0 / (2.0 * heights)


def is_odd():
    return lax.rem(lax.axis_index("depth"), 2) == 1


def strain_of(wx, wz, lo_x, hi_x, lo_z, hi_z, inverse, row):
    def ddx(v):
        return (pltpu.roll(v, 127, 1) - pltpu.roll(v, 1, 1)) * 0.5

    def ddz(v, lo, hi):
        after = jnp.where(row == 7, hi, pltpu.roll(v, 7, 0))
        before = jnp.where(row == 0, lo, pltpu.roll(v, 1, 0))
        return (after - before) * inverse

    return ddx(wx), ddz(wz, lo_z, hi_z), 0.5 * (ddz(wx, lo_x, hi_x) + ddx(wz))


def wide(row):
    return jnp.broadcast_to(row, (8, 128))


def store_edges(slabs, at, odd, first_ref, second_ref):
    count = slabs.shape[0]
    top, bottom = slabs[:, 0, :], slabs[:, 7, :]
    first_ref[at : at + count] = jnp.where(odd, top, bottom).astype(BF16)
    second_ref[at : at + count] = jnp.where(odd, bottom, top).astype(BF16)


def begin_kernel(pair_ref, at_ref, displace_ref, first_ref, second_ref, out_ref):
    rounds, comps, steps = displace_ref.shape[:3]
    odd = is_odd()
    for k in range(rounds):
        for c in range(comps):
            slabs = displace_ref[k, c].astype(F32)
            store_edges(slabs, (k * comps + c) * steps, odd, first_ref, second_ref)
            for t in range(steps):
                out_ref[k * steps + t, c] = displace_ref[k, c, t]
    row = lax.broadcasted_iota(jnp.int32, (8, 128), 0)
    lane = lax.broadcasted_iota(jnp.int32, (8, 128), 1)
    for k in range(rounds):
        extra = jnp.zeros((8, 128), F32)
        for r in range(pair_ref.shape[1]):
            slot = at_ref[k, pair_ref[k, r]].astype(F32)
            extra = jnp.where((row == 4) & (lane == r), slot, extra)
        for t in range(steps):
            out_ref[k * steps + t, 2] = extra.astype(BF16)


def halos_kernel(first_ref, second_ref, in_ref, out_ref, *, rounds, comps):
    steps = in_ref.shape[0] // rounds
    odd = is_odd()
    row = lax.broadcasted_iota(jnp.int32, (8, 128), 0)
    for k in range(rounds):
        halos = []
        for c in range(comps):
            at = (k * comps + c) * steps
            one, two = first_ref[at : at + steps].astype(F32), second_ref[at : at + steps].astype(F32)
            halos += [jnp.where(odd, one, two), jnp.where(odd, two, one)]
        for t in range(steps):
            p = k * steps + t
            tile = in_ref[p, 2].astype(F32)
            for i, halo in enumerate(halos):
                tile = jnp.where(row == i, wide(halo[t : t + 1]), tile)
            out_ref[p, 2] = tile.astype(BF16)


def select_kernel(in_ref, out_ref, strain_ref, slots_ref, scalars_ref, sem):
    sources, receivers = in_ref.shape[0], out_ref.shape[1] // 3
    for s in range(sources):
        slots_ref[s : s + 1] = in_ref[s, 2].astype(F32)[4:5].astype(jnp.int32)
    copy = pltpu.make_async_copy(slots_ref, scalars_ref, sem)
    copy.start()
    inverse = inverse_spacing()
    row = lax.broadcasted_iota(jnp.int32, (8, 128), 0)

    def strain_step(s, carry):
        tile = in_ref[s, 2].astype(F32)
        halos = [wide(tile[i : i + 1]) for i in range(4)]
        wx, wz = in_ref[s, 0].astype(F32), in_ref[s, 1].astype(F32)
        for c, part in enumerate(strain_of(wx, wz, *halos, inverse, row)):
            strain_ref[s, c] = part.astype(BF16)
        return carry

    lax.fori_loop(0, sources, strain_step, 0, unroll=8)
    copy.wait()

    def select_step(d, carry):
        for r in range(receivers):
            s = scalars_ref[d, r]
            for c in range(3):
                out_ref[d, r * 3 + c] = strain_ref[s, c]
        return carry

    lax.fori_loop(0, sources, select_step, 0, unroll=8)


def green_edges_kernel(green_ref, first_ref, second_ref):
    odd = is_odd()
    for at in range(0, green_ref.shape[0], 8):
        store_edges(green_ref[at : at + 8].astype(F32), at, odd, first_ref, second_ref)


def green_strain_kernel(green_ref, first_ref, second_ref, out_ref):
    pairs, comps, steps = green_ref.shape[:3]
    odd = is_odd()
    inverse = inverse_spacing()
    row = lax.broadcasted_iota(jnp.int32, (8, 128), 0)

    def step(pair, carry):
        halos = []
        for c in range(comps):
            one = first_ref[pair, c].astype(F32)
            two = second_ref[pair, c].astype(F32)
            halos += [jnp.where(odd, one, two), jnp.where(odd, two, one)]
        for t in range(steps):
            rows = [wide(halo[t : t + 1]) for halo in halos]
            wx, wz = green_ref[pair, 0, t].astype(F32), green_ref[pair, 1, t].astype(F32)
            b0, b1, b2 = (b.astype(BF16).astype(F32) for b in strain_of(wx, wz, *rows, inverse, row))
            out_ref[pair, 0, t] = b0 + b1
            out_ref[pair, 1, t] = b0 - b1
            out_ref[pair, 2, t] = b2
        return carry

    lax.fori_loop(0, pairs, step, 0)


def correlate_kernel(source_ref, green_ref, out_ref, buffer_ref, sems):
    rounds, receivers, _, forces = out_ref.shape[:4]
    steps = green_ref.shape[2]

    def leave(k, r):
        i = k * receivers + r
        return pltpu.make_async_copy(buffer_ref.at[i], out_ref.at[k, r], sems.at[i])

    def pair_step(i, carry):
        k, r = i // receivers, lax.rem(i, receivers)
        total, spread, cross = [], [], []
        for t in range(steps):
            a0, a1, a2 = (source_ref[k * steps + t, r * 3 + c].astype(F32) for c in range(3))
            total.append(a0 + a1)
            spread.append(a0 - a1)
            cross.append(a2 * 4.0)
        for f in range(forces):
            g = r * forces + f
            for lag in range(LAGS):
                offset = lag - LAGS // 2
                lam = shear = None
                for t in range(max(0, -offset), min(steps, steps - offset)):
                    u = t + offset
                    x = total[t] * green_ref[g, 0, u]
                    y = spread[t] * green_ref[g, 1, u] + cross[t] * green_ref[g, 2, u]
                    lam = x if lam is None else lam + x
                    shear = y if shear is None else shear + y
                buffer_ref[i, 0, f, lag] = lam.astype(BF16)
                buffer_ref[i, 1, f, lag] = (lam + shear).astype(BF16)
        leave(k, r).start()
        return carry

    lax.fori_loop(0, rounds * receivers, pair_step, 0)
    for i in range(rounds * receivers):
        leave(i // receivers, i % receivers).wait()


def exchange(first, second):
    second = lax.ppermute(second, "depth", NEXT_CHIP)
    first = lax.ppermute(first, "depth", SAME_CHIP)
    return first, second


def shards(displace, green, pair_src, source_at):
    rounds, _, comps, steps, rows, cells = displace.shape
    receivers, forces = green.shape[:2]
    sources = source_at.shape[1]
    assert rounds * steps == lax.axis_size("recv") == sources
    assert (rows, cells, lax.axis_size("depth")) == (8, 128, 4)
    own = rounds * comps * steps
    far = receivers * forces * comps * steps

    first, second, messages = pl.pallas_call(
        begin_kernel,
        out_shape=(
            pltpu.VMEM((own, cells), BF16),
            pltpu.VMEM((own, cells), BF16),
            pltpu.VMEM((sources, 3, rows, cells), BF16),
        ),
        in_specs=[SMEM, SMEM, VMEM],
        out_specs=(VMEM,) * 3,
        name="begin",
    )(pair_src, source_at, displace.reshape(rounds, comps, steps, rows, cells))
    first, second = exchange(first, second)
    messages = pl.pallas_call(
        lambda *refs: halos_kernel(*refs, rounds=rounds, comps=comps),
        out_shape=pltpu.VMEM((sources, 3, rows, cells), BF16),
        in_specs=[VMEM] * 3,
        out_specs=VMEM,
        input_output_aliases={2: 0},
        name="halos",
    )(*pinned(first, second, messages))
    pieces = lax.all_to_all(messages, "recv", 0, 0, tiled=True)

    green_first, green_second = pl.pallas_call(
        green_edges_kernel,
        out_shape=(pltpu.VMEM((far, cells), BF16),) * 2,
        in_specs=[VMEM],
        out_specs=(VMEM,) * 2,
        cost_estimate=pl.CostEstimate(flops=1 << 20, bytes_accessed=1 << 20, transcendentals=0),
        name="green_edges",
    )(green.reshape(far, rows, cells))
    green_first, green_second = exchange(green_first, green_second)
    pairs = receivers * forces
    green_strain = pl.pallas_call(
        green_strain_kernel,
        out_shape=pltpu.VMEM((pairs, 3, steps, rows, cells), F32),
        in_specs=[VMEM] * 3,
        out_specs=VMEM,
        cost_estimate=pl.CostEstimate(flops=1 << 23, bytes_accessed=1 << 20, transcendentals=0),
        name="green_strain",
    )(
        green.reshape(pairs, comps, steps, rows, cells),
        *pinned(*(a.reshape(pairs, comps, steps, cells) for a in (green_first, green_second))),
    )

    chosen = pl.pallas_call(
        select_kernel,
        out_shape=pltpu.VMEM((sources, receivers * 3, rows, cells), BF16),
        in_specs=[VMEM],
        out_specs=VMEM,
        scratch_shapes=[
            pltpu.VMEM((sources, 3, rows, cells), BF16),
            pltpu.VMEM((sources, cells), jnp.int32),
            pltpu.SMEM((sources, cells), jnp.int32),
            pltpu.SemaphoreType.DMA,
        ],
        name="select",
    )(*pinned(pieces))
    paired = lax.all_to_all(chosen, "recv", 0, 0, tiled=True)
    result = (2, forces, LAGS, rows, cells)
    return pl.pallas_call(
        correlate_kernel,
        out_shape=jax.ShapeDtypeStruct((rounds, receivers, *result), BF16),
        in_specs=[VMEM] * 2,
        out_specs=ANY,
        scratch_shapes=[
            pltpu.VMEM((rounds * receivers, *result), BF16),
            pltpu.SemaphoreType.DMA((rounds * receivers,)),
        ],
        name="correlate",
    )(*pinned(paired, green_strain))


def solution(mesh):
    return jax.shard_map(
        shards,
        mesh=mesh,
        in_specs=(
            P(None, "recv", None, None, "depth", None),
            P("recv", None, None, None, "depth", None),
            P(None, "recv"),
            P(),
        ),
        out_specs=P(None, "recv", None, None, None, "depth", None),
        check_vma=False,
    )
```

time: 58.6 us -> 45.7 us (0.78)
  blocking collectives: 33.8 us -> 17.7 us
  Pallas kernels: 16.1 us -> 8.33 us
  starting transfers between devices: 2.41 us -> 8.41 us
  waiting for transfers between devices: 4.68 us -> 10.4 us
  local copies, waits for them, and re-layouts: 0.62 us -> 0 us
    all_to_all x2 -> x1, blocking collectives: 33.8 us -> 17.7 us  [shards(): pieces = lax.all_to_all(messages, 'recv', 0, 0, tiled=True)]
    pallas_call x4 -> x6, Pallas kernels: 16.1 us -> 8.33 us  [the longest x1 2.46 us: shards(): pl.pallas_call(correlate_kernel, out_shape=jax.ShapeDtypeStruct((rounds,...]
    ppermute x2 -> x4, waiting for transfers between devices: 4.68 us -> 8.96 us  [the longest x2 8.95 us: exchange(): second = lax.ppermute(second, 'depth', NEXT_CHIP)]
    all_to_all x0 -> x1, starting transfers between devices: none -> 3.92 us  [shards(): paired = lax.all_to_all(chosen, 'recv', 0, 0, tiled=True)]
    ppermute x2 -> x4, starting transfers between devices: 2.41 us -> 4.48 us  [the longest x2 4.31 us: exchange(): second = lax.ppermute(second, 'depth', NEXT_CHIP)]
    all_to_all x0 -> x1, waiting for transfers between devices: none -> 1.42 us  [shards(): paired = lax.all_to_all(chosen, 'recv', 0, 0, tiled=True)]
    unnamed x4 -> x0, local copies, waits for them, and re-layouts: 0.62 us -> none
  transfers between devices with their start and end apart: 2 -> 5, of which waited for: 1 -> 3; matrix products, arithmetic and copies ran while one was open for 0% -> 0% of each run, Pallas kernels for 0% -> 6%
where the time goes in v2:
time: 45.7 us; the launch traced here: 44.9 us
  blocking collectives  17.7 us (39%)
  waiting for transfers between devices  10.4 us (23%)
  starting transfers between devices  8.41 us (18%)
  Pallas kernels  8.33 us (18%)
    all_to_all x1, blocking collectives, shards(): pieces = lax.all_to_all(messages, 'recv', 0, 0, tiled=True)  17.7 us
    ppermute x2, waiting for transfers between devices, exchange(): second = lax.ppermute(second, 'depth', NEXT_CHIP)  8.95 us
    ppermute x2, starting transfers between devices, exchange(): second = lax.ppermute(second, 'depth', NEXT_CHIP)  4.31 us
    all_to_all x1, starting transfers between devices, shards(): paired = lax.all_to_all(chosen, 'recv', 0, 0, tiled=True)  3.92 us
    pallas_call x1, Pallas kernels, shards(): pl.pallas_call(correlate_kernel, out_shape=jax.ShapeDtypeStruct((rounds,...  2.46 us
    pallas_call x1, Pallas kernels, shards(): pl.pallas_call(select_kernel, out_shape=pltpu.VMEM((sources, receivers *...  1.88 us
    pallas_call x1, Pallas kernels, shards(): pl.pallas_call(green_strain_kernel, out_shape=pltpu.VMEM((pairs, 3, steps...  1.72 us
    all_to_all x1, waiting for transfers between devices, shards(): paired = lax.all_to_all(chosen, 'recv', 0, 0, tiled=True)  1.42 us
  transfers between devices with their start and end apart: 5, of which 3 were waited for; matrix products, arithmetic and copies ran while one was open for 0% of the time, Pallas kernels for 6%

profile of v2, /device:TPU:4, one launch (start us, length us, event | category | flops | bytes accessed | tf_op | source)
XLA Modules:
  0.0 44.9 jit_solution(710540870467135148)
XLA Ops:
  0.0 1.0 %begin.1 = (bf16[64,128]{1,0:T(8,128)(2,1)S(1)}, bf16[64,128]{1,0:T(8,128)(2,1)S(1)}, bf16[32,3,8,128]{3,2,1,0:T(8,128)(2,1)S(1)}) custom-call(s32[4,4]{1,0:T(4,128)} %pair_ref.1, s32[4,32]{1,0:T(4,128)} %at_ref.1, bf16[4,2,8,8,128]{4,3,2,1,0:T(8,128)(2,1)} %bitcast.9), custom_call_target="tpu_custom_call" | custom-call | tf_op jit(solution)/shard_map/begin/pallas_call | solution.py:207
  1.1 0.1 collective-permute-start
  1.1 2.4 %collective-permute-start.1 = (bf16[64,128]{1,0:T(8,128)(2,1)S(1)}, bf16[64,128]{1,0:T(8,128)(2,1)S(1)}, u32[]{:S(2)}, u32[]{:S(2)}) collective-permute-start(bf16[64,128]{1,0:T(8,128)(2,1)S(1)} %get-tuple-element.11), channel_id=1, source_target_pairs={{1,2},{2,1},{5,6},{6,5},{9,10},{10,9},{13,14},{14,13},{17,18},{18,... | collective-permute-start | bytes 49160 | tf_op jit(solution)/shard_map/ppermute | solution.py:193
  3.5 0.0 collective-permute-done.refs_0_
  3.6 4.2 %collective-permute-done.1.refs_1_ = bf16[64,128]{1,0:T(8,128)(2,1)S(1)} collective-permute-done((bf16[64,128]{1,0:T(8,128)(2,1)S(1)}, bf16[64,128]{1,0:T(8,128)(2,1)S(1)}, u32[]{:S(2)}, u32[]{:S(2)}) %collective-permute-start.1) | collective-permute-done | bytes 16416 | tf_op jit(solution)/shard_map/ppermute | solution.py:193
  7.7 0.1 halos.1
  7.8 17.7 %all_to_all.10.in_ref = bf16[32,3,8,128]{3,2,1,0:T(8,128)(2,1)S(1)} all-to-all(bf16[32,3,8,128]{3,2,1,0:T(8,128)(2,1)S(1)} %halos.1), channel_id=1, replica_groups=mesh['recv'=32,'depth'=4] {'recv'}, dimensions={0} | all-to-all | bytes 393216 | tf_op jit(solution)/shard_map/all_to_all | solution.py:227
  25.5 1.9 %select.1 = bf16[32,12,8,128]{3,2,1,0:T(8,128)(2,1)} custom-call(bf16[32,3,8,128]{3,2,1,0:T(8,128)(2,1)S(1)} %all_to_all.10.in_ref), custom_call_target="tpu_custom_call" | custom-call | tf_op jit(solution)/shard_map/select/pallas_call | solution.py:251
  27.3 3.9 %all-to-all-start.1 = ((bf16[32,12,8,128]{3,2,1,0:T(8,128)(2,1)}), bf16[32,12,8,128]{3,2,1,0:T(8,128)(2,1)S(1)}, u32[]{:S(2)}, u32[]{:S(2)}) async-start(bf16[32,12,8,128]{3,2,1,0:T(8,128)(2,1)} %select.1), calls=%async_computation.1 | async-start | bytes 1572864 | tf_op jit(solution)/shard_map/all_to_all | solution.py:264
  31.3 1.2 %green_edges.1 = (bf16[128,128]{1,0:T(8,128)(2,1)S(1)}, bf16[128,128]{1,0:T(8,128)(2,1)S(1)}) custom-call(bf16[128,8,128]{2,1,0:T(8,128)(2,1)} %bitcast.7), custom_call_target="tpu_custom_call" | custom-call | flops 1048576 | bytes 1048576 | tf_op jit(solution)/shard_map/green_edges/pallas_call | solution.py:229
  32.5 0.1 collective-permute-start.2
  32.5 1.9 %collective-permute-start.3 = (bf16[128,128]{1,0:T(8,128)(2,1)S(1)}, bf16[128,128]{1,0:T(8,128)(2,1)S(1)}, u32[]{:S(2)}, u32[]{:S(2)}) collective-permute-start(bf16[128,128]{1,0:T(8,128)(2,1)S(1)} %get-tuple-element.14), channel_id=1, source_target_pairs={{1,2},{2,1},{5,6},{6,5},{9,10},{10,9},{13,14},{14,13},{17,18},{18,... | collective-permute-start | bytes 98312 | tf_op jit(solution)/shard_map/ppermute | solution.py:193
  34.5 0.0 collective-permute-done.2
  34.5 4.8 %collective-permute-done.3 = bf16[128,128]{1,0:T(8,128)(2,1)S(1)} collective-permute-done((bf16[128,128]{1,0:T(8,128)(2,1)S(1)}, bf16[128,128]{1,0:T(8,128)(2,1)S(1)}, u32[]{:S(2)}, u32[]{:S(2)}) %collective-permute-start.3) | collective-permute-done | bytes 32800 | tf_op jit(solution)/shard_map/ppermute | solution.py:193
  39.3 1.7 %green_strain.1.green_ref = f32[8,3,8,8,128]{4,3,2,1,0:T(8,128)S(1)} custom-call(bf16[8,2,8,8,128]{4,3,2,1,0:T(8,128)(2,1)} %bitcast.8, bf16[8,2,8,128]{3,2,1,0:T(8,128)(2,1)S(1)} %bitcast.5, bf16[8,2,8,128]{3,2,1,0:T(8,128)(2,1)S(1)} %bitcast.6), custom_call_target="tpu_custom_call" | custom-call | flops 8388608 | bytes 1048576 | tf_op jit(solution)/shard_map/green_strain/pallas_call | solution.py:239
  41.0 1.4 %all-to-all-done.1.source_ref = bf16[32,12,8,128]{3,2,1,0:T(8,128)(2,1)S(1)} async-done(((bf16[32,12,8,128]{3,2,1,0:T(8,128)(2,1)}), bf16[32,12,8,128]{3,2,1,0:T(8,128)(2,1)S(1)}, u32[]{:S(2)}, u32[]{:S(2)}) %all-to-all-start.1) | async-done | bytes 786464 | tf_op jit(solution)/shard_map/all_to_all | solution.py:264
  42.4 2.5 %correlate.1 = bf16[4,4,2,2,9,8,128]{6,5,4,3,2,1,0:T(8,128)(2,1)} custom-call(bf16[32,12,8,128]{3,2,1,0:T(8,128)(2,1)S(1)} %all-to-all-done.1.source_ref, f32[8,3,8,8,128]{4,3,2,1,0:T(8,128)S(1)} %green_strain.1.green_ref), custom_call_target="tpu_custom_call" | custom-call | tf_op jit(solution)/shard_map/correlate/pallas_call | solution.py:266
Async XLA Ops:
  1.1 2.5 %collective-permute-start = (bf16[64,128]{1,0:T(8,128)(2,1)S(1)}, bf16[64,128]{1,0:T(8,128)(2,1)S(1)}, u32[]{:S(2)}, u32[]{:S(2)}) collective-permute-start(bf16[64,128]{1,0:T(8,128)(2,1)S(1)} %get-tuple-element.10), channel_id=1, source_target_pairs={{0,1},{1,0},{2,3},{3,2},{4,5},{5,4},{6,7},{7,6},{8,9},{9,8},{10,11... | collective-permute-start | bytes 49160 | tf_op jit(solution)/shard_map/ppermute | solution.py:194
  1.1 6.6 %collective-permute-start.1 = (bf16[64,128]{1,0:T(8,128)(2,1)S(1)}, bf16[64,128]{1,0:T(8,128)(2,1)S(1)}, u32[]{:S(2)}, u32[]{:S(2)}) collective-permute-start(bf16[64,128]{1,0:T(8,128)(2,1)S(1)} %get-tuple-element.11), channel_id=1, source_target_pairs={{1,2},{2,1},{5,6},{6,5},{9,10},{10,9},{13,14},{14,13},{17,18},{18,... | collective-permute-start | bytes 49160 | tf_op jit(solution)/shard_map/ppermute | solution.py:193
  27.3 15.1 %all-to-all-start.1 = ((bf16[32,12,8,128]{3,2,1,0:T(8,128)(2,1)}), bf16[32,12,8,128]{3,2,1,0:T(8,128)(2,1)S(1)}, u32[]{:S(2)}, u32[]{:S(2)}) async-start(bf16[32,12,8,128]{3,2,1,0:T(8,128)(2,1)} %select.1), calls=%async_computation.1 | async-start | bytes 1572864 | tf_op jit(solution)/shard_map/all_to_all | solution.py:264
  32.5 2.0 %collective-permute-start.2 = (bf16[128,128]{1,0:T(8,128)(2,1)S(1)}, bf16[128,128]{1,0:T(8,128)(2,1)S(1)}, u32[]{:S(2)}, u32[]{:S(2)}) collective-permute-start(bf16[128,128]{1,0:T(8,128)(2,1)S(1)} %get-tuple-element.13), channel_id=1, source_target_pairs={{0,1},{1,0},{2,3},{3,2},{4,5},{5,4},{6,7},{7,6},{8,9},{9,8},{10,11... | collective-permute-start | bytes 98312 | tf_op jit(solution)/shard_map/ppermute | solution.py:194
  32.5 6.7 %collective-permute-start.3 = (bf16[128,128]{1,0:T(8,128)(2,1)S(1)}, bf16[128,128]{1,0:T(8,128)(2,1)S(1)}, u32[]{:S(2)}, u32[]{:S(2)}) collective-permute-start(bf16[128,128]{1,0:T(8,128)(2,1)S(1)} %get-tuple-element.14), channel_id=1, source_target_pairs={{1,2},{2,1},{5,6},{6,5},{9,10},{10,9},{13,14},{14,13},{17,18},{18,... | collective-permute-start | bytes 98312 | tf_op jit(solution)/shard_map/ppermute | solution.py:193

commit v3 on v2

--- a/solution.py
+++ b/solution.py
@@ -6,6 +6,8 @@
 from jax.sharding import PartitionSpec as P
 
 LAGS = 9
+FIRST_ORDER = 31
+SECOND_ORDER = 22
 F32 = jnp.float32
 BF16 = jnp.bfloat16
 VMEM = pl.BlockSpec(memory_space=pltpu.VMEM)
@@ -54,7 +56,7 @@
     second_ref[at : at + count] = jnp.where(odd, bottom, top).astype(BF16)
 
 
-def begin_kernel(pair_ref, at_ref, displace_ref, first_ref, second_ref, out_ref):
+def begin_kernel(pair_ref, at_ref, displace_ref, green_ref, first_ref, second_ref, out_ref):
     rounds, comps, steps = displace_ref.shape[:3]
     odd = is_odd()
     for k in range(rounds):
@@ -62,16 +64,19 @@
             slabs = displace_ref[k, c].astype(F32)
             store_edges(slabs, (k * comps + c) * steps, odd, first_ref, second_ref)
             for t in range(steps):
-                out_ref[k * steps + t, c] = displace_ref[k, c, t]
+                out_ref[(k * steps + t) ^ FIRST_ORDER, c] = displace_ref[k, c, t]
+    base = rounds * comps * steps
+    for at in range(0, green_ref.shape[0], 8):
+        store_edges(green_ref[at : at + 8].astype(F32), base + at, odd, first_ref, second_ref)
     row = lax.broadcasted_iota(jnp.int32, (8, 128), 0)
     lane = lax.broadcasted_iota(jnp.int32, (8, 128), 1)
     for k in range(rounds):
         extra = jnp.zeros((8, 128), F32)
         for r in range(pair_ref.shape[1]):
-            slot = at_ref[k, pair_ref[k, r]].astype(F32)
+            slot = (at_ref[k, pair_ref[k, r]] ^ FIRST_ORDER).astype(F32)
             extra = jnp.where((row == 4) & (lane == r), slot, extra)
         for t in range(steps):
-            out_ref[k * steps + t, 2] = extra.astype(BF16)
+            out_ref[(k * steps + t) ^ FIRST_ORDER, 2] = extra.astype(BF16)
 
 
 def halos_kernel(first_ref, second_ref, in_ref, out_ref, *, rounds, comps):
@@ -85,14 +90,35 @@
             one, two = first_ref[at : at + steps].astype(F32), second_ref[at : at + steps].astype(F32)
             halos += [jnp.where(odd, one, two), jnp.where(odd, two, one)]
         for t in range(steps):
-            p = k * steps + t
+            p = (k * steps + t) ^ FIRST_ORDER
             tile = in_ref[p, 2].astype(F32)
             for i, halo in enumerate(halos):
                 tile = jnp.where(row == i, wide(halo[t : t + 1]), tile)
             out_ref[p, 2] = tile.astype(BF16)
 
 
-def select_kernel(in_ref, out_ref, strain_ref, slots_ref, scalars_ref, sem):
+def green_strain(green_ref, first_ref, second_ref, out_ref, inverse, row):
+    pairs, comps, steps = green_ref.shape[:3]
+    skip = first_ref.shape[0] - pairs * comps * steps
+    odd = is_odd()
+
+    def step(pair, carry):
+        halos = []
+        for c in range(comps):
+            at = pl.multiple_of(skip + (pair * comps + c) * steps, steps)
+            one, two = first_ref[pl.ds(at, steps)].astype(F32), second_ref[pl.ds(at, steps)].astype(F32)
+            halos += [jnp.where(odd, one, two), jnp.where(odd, two, one)]
+        for t in range(steps):
+            rows = [wide(halo[t : t + 1]) for halo in halos]
+            wx, wz = green_ref[pair, 0, t].astype(F32), green_ref[pair, 1, t].astype(F32)
+            for c, part in enumerate(strain_of(wx, wz, *rows, inverse, row)):
+                out_ref[pair, c, t] = part.astype(BF16)
+        return carry
+
+    lax.fori_loop(0, pairs, step, 0)
+
+
+def select_kernel(in_ref, green_ref, first_ref, second_ref, out_ref, green_out_ref, strain_ref, slots_ref, scalars_ref, sem):
     sources, receivers = in_ref.shape[0], out_ref.shape[1] // 3
     for s in range(sources):
         slots_ref[s : s + 1] = in_ref[s, 2].astype(F32)[4:5].astype(jnp.int32)
@@ -110,11 +136,12 @@
         return carry
 
     lax.fori_loop(0, sources, strain_step, 0, unroll=8)
+    green_strain(green_ref, first_ref, second_ref, green_out_ref, inverse, row)
     copy.wait()
 
     def select_step(d, carry):
         for r in range(receivers):
-            s = scalars_ref[d, r]
+            s = scalars_ref[d ^ (FIRST_ORDER ^ SECOND_ORDER), r]
             for c in range(3):
                 out_ref[d, r * 3 + c] = strain_ref[s, c]
         return carry
@@ -122,39 +149,19 @@
     lax.fori_loop(0, sources, select_step, 0, unroll=8)
 
 
-def green_edges_kernel(green_ref, first_ref, second_ref):
-    odd = is_odd()
-    for at in range(0, green_ref.shape[0], 8):
-        store_edges(green_ref[at : at + 8].astype(F32), at, odd, first_ref, second_ref)
-
-
-def green_strain_kernel(green_ref, first_ref, second_ref, out_ref):
-    pairs, comps, steps = green_ref.shape[:3]
-    odd = is_odd()
-    inverse = inverse_spacing()
-    row = lax.broadcasted_iota(jnp.int32, (8, 128), 0)
-
-    def step(pair, carry):
-        halos = []
-        for c in range(comps):
-            one = first_ref[pair, c].astype(F32)
-            two = second_ref[pair, c].astype(F32)
-            halos += [jnp.where(odd, one, two), jnp.where(odd, two, one)]
-        for t in range(steps):
-            rows = [wide(halo[t : t + 1]) for halo in halos]
-            wx, wz = green_ref[pair, 0, t].astype(F32), green_ref[pair, 1, t].astype(F32)
-            b0, b1, b2 = (b.astype(BF16).astype(F32) for b in strain_of(wx, wz, *rows, inverse, row))
-            out_ref[pair, 0, t] = b0 + b1
-            out_ref[pair, 1, t] = b0 - b1
-            out_ref[pair, 2, t] = b2
-        return carry
-
-    lax.fori_loop(0, pairs, step, 0)
-
-
-def correlate_kernel(source_ref, green_ref, out_ref, buffer_ref, sems):
+def correlate_kernel(source_ref, strain_ref, out_ref, green_ref, buffer_ref, sems):
     rounds, receivers, _, forces = out_ref.shape[:4]
     steps = green_ref.shape[2]
+
+    def widen(g, carry):
+        for t in range(steps):
+            b0, b1, b2 = (strain_ref[g, c, t].astype(F32) for c in range(3))
+            green_ref[g, 0, t] = b0 + b1
+            green_ref[g, 1, t] = b0 - b1
+            green_ref[g, 2, t] = b2
+        return carry
+
+    lax.fori_loop(0, receivers * forces, widen, 0)
 
     def leave(k, r):
         i = k * receivers + r
@@ -164,7 +171,7 @@
         k, r = i // receivers, lax.rem(i, receivers)
         total, spread, cross = [], [], []
         for t in range(steps):
-            a0, a1, a2 = (source_ref[k * steps + t, r * 3 + c].astype(F32) for c in range(3))
+            a0, a1, a2 = (source_ref[(k * steps + t) ^ SECOND_ORDER, r * 3 + c].astype(F32) for c in range(3))
             total.append(a0 + a1)
             spread.append(a0 - a1)
             cross.append(a2 * 4.0)
@@ -195,6 +202,11 @@
     return first, second
 
 
+def exchange_all(messages, order):
+    groups = [[i ^ order for i in range(messages.shape[0])]]
+    return lax.all_to_all(messages, "recv", 0, 0, tiled=True, axis_index_groups=groups)
+
+
 def shards(displace, green, pair_src, source_at):
     rounds, _, comps, steps, rows, cells = displace.shape
     receivers, forces = green.shape[:2]
@@ -207,14 +219,14 @@
     first, second, messages = pl.pallas_call(
         begin_kernel,
         out_shape=(
-            pltpu.VMEM((own, cells), BF16),
-            pltpu.VMEM((own, cells), BF16),
+            pltpu.VMEM((own + far, cells), BF16),
+            pltpu.VMEM((own + far, cells), BF16),
             pltpu.VMEM((sources, 3, rows, cells), BF16),
         ),
-        in_specs=[SMEM, SMEM, VMEM],
+        in_specs=[SMEM, SMEM, VMEM, VMEM],
         out_specs=(VMEM,) * 3,
         name="begin",
-    )(pair_src, source_at, displace.reshape(rounds, comps, steps, rows, cells))
+    )(pair_src, source_at, displace.reshape(rounds, comps, steps, rows, cells), green.reshape(far, rows, cells))
     first, second = exchange(first, second)
     messages = pl.pallas_call(
         lambda *refs: halos_kernel(*refs, rounds=rounds, comps=comps),
@@ -224,35 +236,17 @@
         input_output_aliases={2: 0},
         name="halos",
     )(*pinned(first, second, messages))
-    pieces = lax.all_to_all(messages, "recv", 0, 0, tiled=True)
-
-    green_first, green_second = pl.pallas_call(
-        green_edges_kernel,
-        out_shape=(pltpu.VMEM((far, cells), BF16),) * 2,
-        in_specs=[VMEM],
+    pieces = exchange_all(messages, FIRST_ORDER)
+
+    pairs = receivers * forces
+    chosen, strain = pl.pallas_call(
+        select_kernel,
+        out_shape=(
+            pltpu.VMEM((sources, receivers * 3, rows, cells), BF16),
+            pltpu.VMEM((pairs, 3, steps, rows, cells), BF16),
+        ),
+        in_specs=[VMEM] * 4,
         out_specs=(VMEM,) * 2,
-        cost_estimate=pl.CostEstimate(flops=1 << 20, bytes_accessed=1 << 20, transcendentals=0),
-        name="green_edges",
-    )(green.reshape(far, rows, cells))
-    green_first, green_second = exchange(green_first, green_second)
-    pairs = receivers * forces
-    green_strain = pl.pallas_call(
-        green_strain_kernel,
-        out_shape=pltpu.VMEM((pairs, 3, steps, rows, cells), F32),
-        in_specs=[VMEM] * 3,
-        out_specs=VMEM,
-        cost_estimate=pl.CostEstimate(flops=1 << 23, bytes_accessed=1 << 20, transcendentals=0),
-        name="green_strain",
-    )(
-        green.reshape(pairs, comps, steps, rows, cells),
-        *pinned(*(a.reshape(pairs, comps, steps, cells) for a in (green_first, green_second))),
-    )
-
-    chosen = pl.pallas_call(
-        select_kernel,
-        out_shape=pltpu.VMEM((sources, receivers * 3, rows, cells), BF16),
-        in_specs=[VMEM],
-        out_specs=VMEM,
         scratch_shapes=[
             pltpu.VMEM((sources, 3, rows, cells), BF16),
             pltpu.VMEM((sources, cells), jnp.int32),
@@ -260,8 +254,8 @@
             pltpu.SemaphoreType.DMA,
         ],
         name="select",
-    )(*pinned(pieces))
-    paired = lax.all_to_all(chosen, "recv", 0, 0, tiled=True)
+    )(*pinned(pieces, green.reshape(pairs, comps, steps, rows, cells), first, second))
+    paired = exchange_all(chosen, SECOND_ORDER)
     result = (2, forces, LAGS, rows, cells)
     return pl.pallas_call(
         correlate_kernel,
@@ -269,11 +263,12 @@
         in_specs=[VMEM] * 2,
         out_specs=ANY,
         scratch_shapes=[
+            pltpu.VMEM((pairs, 3, steps, rows, cells), F32),
             pltpu.VMEM((rounds * receivers, *result), BF16),
             pltpu.SemaphoreType.DMA((rounds * receivers,)),
         ],
         name="correlate",
-    )(*pinned(paired, green_strain))
+    )(*pinned(paired, strain))
 
 
 def solution(mesh):

time: 45.7 us -> 41.8 us (0.915); the launches traced: 44.9 us -> 41.6 us
  blocking collectives: 17.7 us -> 29.2 us
  starting transfers between devices: 8.41 us -> 2.48 us
  waiting for transfers between devices: 10.4 us -> 4.5 us
  Pallas kernels: 8.33 us -> 5.41 us
    all_to_all x1 -> x2, blocking collectives: 17.7 us -> 29.2 us  [exchange_all(): lax.all_to_all(messages, 'recv', 0, 0, tiled=True, axis_index_groups=groups)]
    ppermute x2 -> x1, waiting for transfers between devices: 8.95 us -> 4.5 us  [exchange(): second = lax.ppermute(second, 'depth', NEXT_CHIP)]
    all_to_all x1 -> x0, starting transfers between devices: 3.92 us -> none  [shards(): paired = lax.all_to_all(chosen, 'recv', 0, 0, tiled=True)]
    pallas_call x4 -> x2, Pallas kernels: 5.81 us -> 2.75 us  [the longest x1 1.41 us: shards(): pl.pallas_call(begin_kernel, out_shape=(pltpu.VMEM((own + far, cells), BF...]
    ppermute x2 -> x1, starting transfers between devices: 4.31 us -> 2.39 us  [exchange(): second = lax.ppermute(second, 'depth', NEXT_CHIP)]
    all_to_all x1 -> x0, waiting for transfers between devices: 1.42 us -> none  [shards(): paired = lax.all_to_all(chosen, 'recv', 0, 0, tiled=True)]
  transfers between devices with their start and end apart: 5 -> 2, of which waited for: 3 -> 1; matrix products, arithmetic and copies ran while one was open for 0% -> 0% of each run, Pallas kernels for 6% -> 0%
where the time goes in v3:
time: 41.8 us; the launch traced here: 41.6 us
  blocking collectives  29.2 us (70%)
  Pallas kernels  5.41 us (13%)
  waiting for transfers between devices  4.5 us (11%)
  starting transfers between devices  2.48 us (6%)
    all_to_all x2, blocking collectives, exchange_all(): lax.all_to_all(messages, 'recv', 0, 0, tiled=True, axis_index_groups=groups)  29.2 us
    ppermute x1, waiting for transfers between devices, exchange(): second = lax.ppermute(second, 'depth', NEXT_CHIP)  4.5 us
    pallas_call x1, Pallas kernels, shards(): pl.pallas_call(correlate_kernel, out_shape=jax.ShapeDtypeStruct((rounds,...  2.6 us
    ppermute x1, starting transfers between devices, exchange(): second = lax.ppermute(second, 'depth', NEXT_CHIP)  2.39 us
    pallas_call x1, Pallas kernels, shards(): pl.pallas_call(begin_kernel, out_shape=(pltpu.VMEM((own + far, cells), BF...  1.41 us
    pallas_call x1, Pallas kernels, shards(): pl.pallas_call(select_kernel, out_shape=(pltpu.VMEM((sources, receivers *...  1.34 us
  transfers between devices with their start and end apart: 2, of which 1 were waited for; matrix products, arithmetic and copies ran while one was open for 0% of the time, Pallas kernels for 0%

profile of v3, /device:TPU:4, one launch (start us, length us, event | category | flops | bytes accessed | tf_op | source)
XLA Modules:
  0.0 41.6 jit_solution(12488630505794311949)
XLA Ops:
  0.0 0.0 copy-start
  0.0 1.4 %begin.1 = (bf16[192,128]{1,0:T(8,128)(2,1)S(1)}, bf16[192,128]{1,0:T(8,128)(2,1)S(1)}, bf16[32,3,8,128]{3,2,1,0:T(8,128)(2,1)S(1)}) custom-call(s32[4,4]{1,0:T(4,128)} %pair_ref.1, s32[4,32]{1,0:T(4,128)} %at_ref.1, bf16[4,2,8,8,128]{4,3,2,1,0:T(8,128)(2,1)} %bitcast.5, bf16[128,8,128]{2,1,0:T(8,128)(2,1)} %bitcast.3), custom_call_target="tpu_custom_call" | custom-call | tf_op jit(solution)/shard_map/begin/pallas_call | solution.py:219
  1.4 0.1 collective-permute-start
  1.5 2.4 %collective-permute-start.1 = (bf16[192,128]{1,0:T(8,128)(2,1)S(1)}, bf16[192,128]{1,0:T(8,128)(2,1)S(1)}, u32[]{:S(2)}, u32[]{:S(2)}) collective-permute-start(bf16[192,128]{1,0:T(8,128)(2,1)S(1)} %get-tuple-element.11), channel_id=1, source_target_pairs={{1,2},{2,1},{5,6},{6,5},{9,10},{10,9},{13,14},{14,13},{17,18},{18,... | collective-permute-start | bytes 147464 | tf_op jit(solution)/shard_map/ppermute | solution.py:200
  3.9 0.0 collective-permute-done.refs_0_.first_ref
  3.9 4.5 %collective-permute-done.1.refs_1_.second_ref = bf16[192,128]{1,0:T(8,128)(2,1)S(1)} collective-permute-done((bf16[192,128]{1,0:T(8,128)(2,1)S(1)}, bf16[192,128]{1,0:T(8,128)(2,1)S(1)}, u32[]{:S(2)}, u32[]{:S(2)}) %collective-permute-start.1) | collective-permute-done | bytes 49184 | tf_op jit(solution)/shard_map/ppermute | solution.py:200
  8.4 0.1 halos.1
  8.5 14.7 %all_to_all.10.in_ref = bf16[32,3,8,128]{3,2,1,0:T(8,128)(2,1)S(1)} all-to-all(bf16[32,3,8,128]{3,2,1,0:T(8,128)(2,1)S(1)} %halos.1), channel_id=1, replica_groups={{124,120,116,112,108,104,100,96,92,88,84,80,76,72,68,64,60,56,52,48,44,..., dimensions={0} | all-to-all | bytes 393216 | tf_op jit(solution)/shard_map/all_to_all | solution.py:207
  23.2 0.0 copy-done
  23.2 1.3 %select.1 = (bf16[32,12,8,128]{3,2,1,0:T(8,128)(2,1)S(1)}, bf16[8,3,8,8,128]{4,3,2,1,0:T(8,128)(2,1)S(1)}) custom-call(bf16[32,3,8,128]{3,2,1,0:T(8,128)(2,1)S(1)} %all_to_all.10.in_ref, bf16[8,2,8,8,128]{4,3,2,1,0:T(8,128)(2,1)S(1)} %bitcast.4, bf16[192,128]{1,0:T(8,128)(2,1)S(1)} %collective-permute-done.refs_0_.first_ref, ...), custom_call_target="tpu_custom_call" | custom-call | tf_op jit(solution)/shard_map/select/pallas_call | solution.py:242
  24.5 14.5 %all_to_all.11.source_ref = bf16[32,12,8,128]{3,2,1,0:T(8,128)(2,1)S(1)} all-to-all(bf16[32,12,8,128]{3,2,1,0:T(8,128)(2,1)S(1)} %get-tuple-element.13), channel_id=1, replica_groups={{88,92,80,84,72,76,64,68,120,124,112,116,104,108,96,100,24,28,16,20,8,1..., dimensions={0} | all-to-all | bytes 1572864 | tf_op jit(solution)/shard_map/all_to_all | solution.py:207
  39.0 2.6 %correlate.1 = bf16[4,4,2,2,9,8,128]{6,5,4,3,2,1,0:T(8,128)(2,1)} custom-call(bf16[32,12,8,128]{3,2,1,0:T(8,128)(2,1)S(1)} %all_to_all.11.source_ref, bf16[8,3,8,8,128]{4,3,2,1,0:T(8,128)(2,1)S(1)} %get-tuple-element.14.strain_ref), custom_call_target="tpu_custom_call" | custom-call | tf_op jit(solution)/shard_map/correlate/pallas_call | solution.py:260
Async XLA Ops:
  0.0 23.2 %copy-start = (bf16[4,2,2,8,8,128]{5,4,3,2,1,0:T(8,128)(2,1)S(1)}, bf16[4,2,2,8,8,128]{5,4,3,2,1,0:T(8,128)(2,1)}, u32[]{:S(2)}) copy-start(bf16[4,2,2,8,8,128]{5,4,3,2,1,0:T(8,128)(2,1)} %param.5) | copy-start | bytes 786436
  1.4 2.5 %collective-permute-start = (bf16[192,128]{1,0:T(8,128)(2,1)S(1)}, bf16[192,128]{1,0:T(8,128)(2,1)S(1)}, u32[]{:S(2)}, u32[]{:S(2)}) collective-permute-start(bf16[192,128]{1,0:T(8,128)(2,1)S(1)} %get-tuple-element.10), channel_id=1, source_target_pairs={{0,1},{1,0},{2,3},{3,2},{4,5},{5,4},{6,7},{7,6},{8,9},{9,8},{10,11... | collective-permute-start | bytes 147464 | tf_op jit(solution)/shard_map/ppermute | solution.py:201
  1.5 6.9 %collective-permute-start.1 = (bf16[192,128]{1,0:T(8,128)(2,1)S(1)}, bf16[192,128]{1,0:T(8,128)(2,1)S(1)}, u32[]{:S(2)}, u32[]{:S(2)}) collective-permute-start(bf16[192,128]{1,0:T(8,128)(2,1)S(1)} %get-tuple-element.11), channel_id=1, source_target_pairs={{1,2},{2,1},{5,6},{6,5},{9,10},{10,9},{13,14},{14,13},{17,18},{18,... | collective-permute-start | bytes 147464 | tf_op jit(solution)/shard_map/ppermute | solution.py:200

commit v4 on v3

--- a/solution.py
+++ b/solution.py
@@ -49,25 +49,21 @@
     return jnp.broadcast_to(row, (8, 128))
 
 
-def store_edges(slabs, at, odd, first_ref, second_ref):
-    count = slabs.shape[0]
-    top, bottom = slabs[:, 0, :], slabs[:, 7, :]
-    first_ref[at : at + count] = jnp.where(odd, top, bottom).astype(BF16)
-    second_ref[at : at + count] = jnp.where(odd, bottom, top).astype(BF16)
-
-
-def begin_kernel(pair_ref, at_ref, displace_ref, green_ref, first_ref, second_ref, out_ref):
+def edges_kernel(displace_ref, green_ref, first_ref, second_ref, wide_ref):
+    height = displace_ref.shape[1]
+    near = jnp.where(is_odd(), 0, height - 1)
+    base = 0
+    for ref in (displace_ref, green_ref):
+        for at in range(0, ref.shape[0], 8):
+            start = (base + at) * height
+            wide_ref[start : start + 8 * height] = ref[at : at + 8].astype(F32).reshape(8 * height, -1)
+            for side, out_ref in ((near, first_ref), (height - 1 - near, second_ref)):
+                out_ref[base + at : base + at + 8] = wide_ref[pl.ds(start + side, 8, stride=height)].astype(BF16)
+        base += ref.shape[0]
+
+
+def pack_kernel(pair_ref, at_ref, displace_ref, out_ref):
     rounds, comps, steps = displace_ref.shape[:3]
-    odd = is_odd()
-    for k in range(rounds):
-        for c in range(comps):
-            slabs = displace_ref[k, c].astype(F32)
-            store_edges(slabs, (k * comps + c) * steps, odd, first_ref, second_ref)
-            for t in range(steps):
-                out_ref[(k * steps + t) ^ FIRST_ORDER, c] = displace_ref[k, c, t]
-    base = rounds * comps * steps
-    for at in range(0, green_ref.shape[0], 8):
-        store_edges(green_ref[at : at + 8].astype(F32), base + at, odd, first_ref, second_ref)
     row = lax.broadcasted_iota(jnp.int32, (8, 128), 0)
     lane = lax.broadcasted_iota(jnp.int32, (8, 128), 1)
     for k in range(rounds):
@@ -76,7 +72,10 @@
             slot = (at_ref[k, pair_ref[k, r]] ^ FIRST_ORDER).astype(F32)
             extra = jnp.where((row == 4) & (lane == r), slot, extra)
         for t in range(steps):
-            out_ref[(k * steps + t) ^ FIRST_ORDER, 2] = extra.astype(BF16)
+            p = (k * steps + t) ^ FIRST_ORDER
+            for c in range(comps):
+                out_ref[p, c] = displace_ref[k, c, t]
+            out_ref[p, 2] = extra.astype(BF16)
 
 
 def halos_kernel(first_ref, second_ref, in_ref, out_ref, *, rounds, comps):
@@ -216,18 +215,24 @@
     own = rounds * comps * steps
     far = receivers * forces * comps * steps
 
-    first, second, messages = pl.pallas_call(
-        begin_kernel,
-        out_shape=(
-            pltpu.VMEM((own + far, cells), BF16),
-            pltpu.VMEM((own + far, cells), BF16),
-            pltpu.VMEM((sources, 3, rows, cells), BF16),
-        ),
-        in_specs=[SMEM, SMEM, VMEM, VMEM],
-        out_specs=(VMEM,) * 3,
-        name="begin",
-    )(pair_src, source_at, displace.reshape(rounds, comps, steps, rows, cells), green.reshape(far, rows, cells))
+    edges = pltpu.VMEM((own + far, cells), BF16)
+    first, second = pl.pallas_call(
+        edges_kernel,
+        out_shape=(edges, edges),
+        in_specs=[VMEM] * 2,
+        out_specs=(VMEM,) * 2,
+        scratch_shapes=[pltpu.VMEM(((own + far) * rows, cells), F32)],
+        name="edges",
+    )(displace.reshape(own, rows, cells), green.reshape(far, rows, cells))
     first, second = exchange(first, second)
+    messages = pl.pallas_call(
+        pack_kernel,
+        out_shape=pltpu.VMEM((sources, 3, rows, cells), BF16),
+        in_specs=[SMEM, SMEM, VMEM],
+        out_specs=VMEM,
+        cost_estimate=pl.CostEstimate(flops=1 << 22, bytes_accessed=1 << 20, transcendentals=0),
+        name="pack",
+    )(pair_src, source_at, displace.reshape(rounds, comps, steps, rows, cells))
     messages = pl.pallas_call(
         lambda *refs: halos_kernel(*refs, rounds=rounds, comps=comps),
         out_shape=pltpu.VMEM((sources, 3, rows, cells), BF16),

time: 41.8 us -> 41.7 us (level)
  waiting for transfers between devices: 4.5 us -> 3.52 us
  Pallas kernels: 5.41 us -> 6.19 us
    ppermute x1, waiting for transfers between devices: 4.5 us -> 3.52 us  [exchange(): second = lax.ppermute(second, 'depth', NEXT_CHIP)]
    pallas_call x1 -> x2, Pallas kernels: 1.41 us -> 2.2 us  [the longest x1 1.22 us: shards(): pl.pallas_call(edges_kernel, out_shape=(edges, edges), in_specs=[VMEM] *...]
  transfers between devices with their start and end apart: 2 -> 2, of which waited for: 1 -> 1; matrix products, arithmetic and copies ran while one was open for 0% -> 0% of each run, Pallas kernels for 0% -> 2%
where the time goes in v4:
time: 41.7 us; the launch traced here: 41.4 us
  blocking collectives  29.2 us (70%)
  Pallas kernels  6.19 us (15%)
  waiting for transfers between devices  3.52 us (8%)
  starting transfers between devices  2.48 us (6%)
    all_to_all x2, blocking collectives, exchange_all(): lax.all_to_all(messages, 'recv', 0, 0, tiled=True, axis_index_groups=groups)  29.2 us
    ppermute x1, waiting for transfers between devices, exchange(): second = lax.ppermute(second, 'depth', NEXT_CHIP)  3.52 us
    pallas_call x1, Pallas kernels, shards(): pl.pallas_call(correlate_kernel, out_shape=jax.ShapeDtypeStruct((rounds,...  2.6 us
    ppermute x1, starting transfers between devices, exchange(): second = lax.ppermute(second, 'depth', NEXT_CHIP)  2.39 us
    pallas_call x1, Pallas kernels, shards(): pl.pallas_call(select_kernel, out_shape=(pltpu.VMEM((sources, receivers *...  1.34 us
    pallas_call x1, Pallas kernels, shards(): pl.pallas_call(edges_kernel, out_shape=(edges, edges), in_specs=[VMEM] *...  1.22 us
    pallas_call x1, Pallas kernels, shards(): pl.pallas_call(pack_kernel, out_shape=pltpu.VMEM((sources, 3, rows, cells...  0.97 us
  transfers between devices with their start and end apart: 2, of which 1 were waited for; matrix products, arithmetic and copies ran while one was open for 0% of the time, Pallas kernels for 2%

profile of v4, /device:TPU:4, one launch (start us, length us, event | category | flops | bytes accessed | tf_op | source)
XLA Modules:
  0.0 41.4 jit_solution(3100241339715607656)
XLA Ops:
  0.0 0.0 copy-start
  0.0 1.2 %edges.1 = (bf16[192,128]{1,0:T(8,128)(2,1)S(1)}, bf16[192,128]{1,0:T(8,128)(2,1)S(1)}) custom-call(bf16[64,8,128]{2,1,0:T(8,128)(2,1)} %bitcast.6, bf16[128,8,128]{2,1,0:T(8,128)(2,1)} %bitcast.4), custom_call_target="tpu_custom_call" | custom-call | tf_op jit(solution)/shard_map/edges/pallas_call | solution.py:219
  1.2 0.1 collective-permute-start
  1.3 2.4 %collective-permute-start.1 = (bf16[192,128]{1,0:T(8,128)(2,1)S(1)}, bf16[192,128]{1,0:T(8,128)(2,1)S(1)}, u32[]{:S(2)}, u32[]{:S(2)}) collective-permute-start(bf16[192,128]{1,0:T(8,128)(2,1)S(1)} %get-tuple-element.10), channel_id=1, source_target_pairs={{1,2},{2,1},{5,6},{6,5},{9,10},{10,9},{13,14},{14,13},{17,18},{18,... | collective-permute-start | bytes 147464 | tf_op jit(solution)/shard_map/ppermute | solution.py:199
  3.7 1.0 %pack.1.refs_2_ = bf16[32,3,8,128]{3,2,1,0:T(8,128)(2,1)S(1)} custom-call(s32[4,4]{1,0:T(4,128)} %pair_ref.1, s32[4,32]{1,0:T(4,128)} %at_ref.1, bf16[4,2,8,8,128]{4,3,2,1,0:T(8,128)(2,1)} %bitcast.7), custom_call_target="tpu_custom_call" | custom-call | flops 4194304 | bytes 1048576 | tf_op jit(solution)/shard_map/pack/pallas_call | solution.py:228
  4.7 0.0 collective-permute-done.refs_0_.first_ref
  4.7 3.5 %collective-permute-done.1.refs_1_.second_ref = bf16[192,128]{1,0:T(8,128)(2,1)S(1)} collective-permute-done((bf16[192,128]{1,0:T(8,128)(2,1)S(1)}, bf16[192,128]{1,0:T(8,128)(2,1)S(1)}, u32[]{:S(2)}, u32[]{:S(2)}) %collective-permute-start.1) | collective-permute-done | bytes 49184 | tf_op jit(solution)/shard_map/ppermute | solution.py:199
  8.2 0.1 halos.1
  8.3 14.7 %all_to_all.10.in_ref = bf16[32,3,8,128]{3,2,1,0:T(8,128)(2,1)S(1)} all-to-all(bf16[32,3,8,128]{3,2,1,0:T(8,128)(2,1)S(1)} %halos.1), channel_id=1, replica_groups={{124,120,116,112,108,104,100,96,92,88,84,80,76,72,68,64,60,56,52,48,44,..., dimensions={0} | all-to-all | bytes 393216 | tf_op jit(solution)/shard_map/all_to_all | solution.py:206
  23.0 0.0 copy-done
  23.0 1.3 %select.1 = (bf16[32,12,8,128]{3,2,1,0:T(8,128)(2,1)S(1)}, bf16[8,3,8,8,128]{4,3,2,1,0:T(8,128)(2,1)S(1)}) custom-call(bf16[32,3,8,128]{3,2,1,0:T(8,128)(2,1)S(1)} %all_to_all.10.in_ref, bf16[8,2,8,8,128]{4,3,2,1,0:T(8,128)(2,1)S(1)} %bitcast.5, bf16[192,128]{1,0:T(8,128)(2,1)S(1)} %collective-permute-done.refs_0_.first_ref, ...), custom_call_target="tpu_custom_call" | custom-call | tf_op jit(solution)/shard_map/select/pallas_call | solution.py:247
  24.4 14.5 %all_to_all.11.source_ref = bf16[32,12,8,128]{3,2,1,0:T(8,128)(2,1)S(1)} all-to-all(bf16[32,12,8,128]{3,2,1,0:T(8,128)(2,1)S(1)} %get-tuple-element.11), channel_id=1, replica_groups={{88,92,80,84,72,76,64,68,120,124,112,116,104,108,96,100,24,28,16,20,8,1..., dimensions={0} | all-to-all | bytes 1572864 | tf_op jit(solution)/shard_map/all_to_all | solution.py:206
  38.8 2.6 %correlate.1 = bf16[4,4,2,2,9,8,128]{6,5,4,3,2,1,0:T(8,128)(2,1)} custom-call(bf16[32,12,8,128]{3,2,1,0:T(8,128)(2,1)S(1)} %all_to_all.11.source_ref, bf16[8,3,8,8,128]{4,3,2,1,0:T(8,128)(2,1)S(1)} %get-tuple-element.12.strain_ref), custom_call_target="tpu_custom_call" | custom-call | tf_op jit(solution)/shard_map/correlate/pallas_call | solution.py:265
Async XLA Ops:
  0.0 23.0 %copy-start = (bf16[4,2,2,8,8,128]{5,4,3,2,1,0:T(8,128)(2,1)S(1)}, bf16[4,2,2,8,8,128]{5,4,3,2,1,0:T(8,128)(2,1)}, u32[]{:S(2)}) copy-start(bf16[4,2,2,8,8,128]{5,4,3,2,1,0:T(8,128)(2,1)} %param.5) | copy-start | bytes 786436
  1.2 3.5 %collective-permute-start = (bf16[192,128]{1,0:T(8,128)(2,1)S(1)}, bf16[192,128]{1,0:T(8,128)(2,1)S(1)}, u32[]{:S(2)}, u32[]{:S(2)}) collective-permute-start(bf16[192,128]{1,0:T(8,128)(2,1)S(1)} %get-tuple-element.9), channel_id=1, source_target_pairs={{0,1},{1,0},{2,3},{3,2},{4,5},{5,4},{6,7},{7,6},{8,9},{9,8},{10,11... | collective-permute-start | bytes 147464 | tf_op jit(solution)/shard_map/ppermute | solution.py:200
  1.3 6.9 %collective-permute-start.1 = (bf16[192,128]{1,0:T(8,128)(2,1)S(1)}, bf16[192,128]{1,0:T(8,128)(2,1)S(1)}, u32[]{:S(2)}, u32[]{:S(2)}) collective-permute-start(bf16[192,128]{1,0:T(8,128)(2,1)S(1)} %get-tuple-element.10), channel_id=1, source_target_pairs={{1,2},{2,1},{5,6},{6,5},{9,10},{10,9},{13,14},{14,13},{17,18},{18,... | collective-permute-start | bytes 147464 | tf_op jit(solution)/shard_map/ppermute | solution.py:199

commit v5 on v4

--- a/solution.py
+++ b/solution.py
@@ -6,7 +6,7 @@
 from jax.sharding import PartitionSpec as P
 
 LAGS = 9
-FIRST_ORDER = 31
+FIRST_ORDER = 23
 SECOND_ORDER = 22
 F32 = jnp.float32
 BF16 = jnp.bfloat16
@@ -110,8 +110,10 @@
         for t in range(steps):
             rows = [wide(halo[t : t + 1]) for halo in halos]
             wx, wz = green_ref[pair, 0, t].astype(F32), green_ref[pair, 1, t].astype(F32)
-            for c, part in enumerate(strain_of(wx, wz, *rows, inverse, row)):
-                out_ref[pair, c, t] = part.astype(BF16)
+            b0, b1, b2 = (b.astype(BF16).astype(F32) for b in strain_of(wx, wz, *rows, inverse, row))
+            out_ref[pair, 0, t] = b0 + b1
+            out_ref[pair, 1, t] = b0 - b1
+            out_ref[pair, 2, t] = b2
         return carry
 
     lax.fori_loop(0, pairs, step, 0)
@@ -148,19 +150,9 @@
     lax.fori_loop(0, sources, select_step, 0, unroll=8)
 
 
-def correlate_kernel(source_ref, strain_ref, out_ref, green_ref, buffer_ref, sems):
+def correlate_kernel(source_ref, green_ref, out_ref, buffer_ref, sems):
     rounds, receivers, _, forces = out_ref.shape[:4]
     steps = green_ref.shape[2]
-
-    def widen(g, carry):
-        for t in range(steps):
-            b0, b1, b2 = (strain_ref[g, c, t].astype(F32) for c in range(3))
-            green_ref[g, 0, t] = b0 + b1
-            green_ref[g, 1, t] = b0 - b1
-            green_ref[g, 2, t] = b2
-        return carry
-
-    lax.fori_loop(0, receivers * forces, widen, 0)
 
     def leave(k, r):
         i = k * receivers + r
@@ -248,7 +240,7 @@
         select_kernel,
         out_shape=(
             pltpu.VMEM((sources, receivers * 3, rows, cells), BF16),
-            pltpu.VMEM((pairs, 3, steps, rows, cells), BF16),
+            pltpu.VMEM((pairs, 3, steps, rows, cells), F32),
         ),
         in_specs=[VMEM] * 4,
         out_specs=(VMEM,) * 2,
@@ -258,6 +250,7 @@
             pltpu.SMEM((sources, cells), jnp.int32),
             pltpu.SemaphoreType.DMA,
         ],
+        compiler_params=pltpu.CompilerParams(vmem_limit_bytes=8 << 20),
         name="select",
     )(*pinned(pieces, green.reshape(pairs, comps, steps, rows, cells), first, second))
     paired = exchange_all(chosen, SECOND_ORDER)
@@ -268,10 +261,10 @@
         in_specs=[VMEM] * 2,
         out_specs=ANY,
         scratch_shapes=[
-            pltpu.VMEM((pairs, 3, steps, rows, cells), F32),
             pltpu.VMEM((rounds * receivers, *result), BF16),
             pltpu.SemaphoreType.DMA((rounds * receivers,)),
         ],
+        compiler_params=pltpu.CompilerParams(vmem_limit_bytes=8 << 20),
         name="correlate",
     )(*pinned(paired, strain))
 

time: 41.7 us -> 41.6 us (level)
  no operation moved by 1% of the time
where the time goes in v5:
time: 41.6 us; the launch traced here: 41.3 us
  blocking collectives  29.2 us (70%)
  Pallas kernels  6.1 us (15%)
  waiting for transfers between devices  3.52 us (8%)
  starting transfers between devices  2.48 us (6%)
    all_to_all x2, blocking collectives, exchange_all(): lax.all_to_all(messages, 'recv', 0, 0, tiled=True, axis_index_groups=groups)  29.2 us
    ppermute x1, waiting for transfers between devices, exchange(): second = lax.ppermute(second, 'depth', NEXT_CHIP)  3.52 us
    pallas_call x1, Pallas kernels, shards(): pl.pallas_call(correlate_kernel, out_shape=jax.ShapeDtypeStruct((rounds,...  2.5 us
    ppermute x1, starting transfers between devices, exchange(): second = lax.ppermute(second, 'depth', NEXT_CHIP)  2.39 us
    pallas_call x1, Pallas kernels, shards(): pl.pallas_call(select_kernel, out_shape=(pltpu.VMEM((sources, receivers *...  1.34 us
    pallas_call x1, Pallas kernels, shards(): pl.pallas_call(edges_kernel, out_shape=(edges, edges), in_specs=[VMEM] *...  1.22 us
    pallas_call x1, Pallas kernels, shards(): pl.pallas_call(pack_kernel, out_shape=pltpu.VMEM((sources, 3, rows, cells...  0.97 us
  transfers between devices with their start and end apart: 2, of which 1 were waited for; matrix products, arithmetic and copies ran while one was open for 0% of the time, Pallas kernels for 2%

profile of v5, /device:TPU:4, one launch (start us, length us, event | category | flops | bytes accessed | tf_op | source)
XLA Modules:
  0.0 41.3 jit_solution(10387053771345010991)
XLA Ops:
  0.0 0.0 copy-start
  0.0 1.2 %edges.1 = (bf16[192,128]{1,0:T(8,128)(2,1)S(1)}, bf16[192,128]{1,0:T(8,128)(2,1)S(1)}) custom-call(bf16[64,8,128]{2,1,0:T(8,128)(2,1)} %bitcast.6, bf16[128,8,128]{2,1,0:T(8,128)(2,1)} %bitcast.4), custom_call_target="tpu_custom_call" | custom-call | tf_op jit(solution)/shard_map/edges/pallas_call | solution.py:211
  1.2 0.1 collective-permute-start
  1.3 2.4 %collective-permute-start.1 = (bf16[192,128]{1,0:T(8,128)(2,1)S(1)}, bf16[192,128]{1,0:T(8,128)(2,1)S(1)}, u32[]{:S(2)}, u32[]{:S(2)}) collective-permute-start(bf16[192,128]{1,0:T(8,128)(2,1)S(1)} %get-tuple-element.10), channel_id=1, source_target_pairs={{1,2},{2,1},{5,6},{6,5},{9,10},{10,9},{13,14},{14,13},{17,18},{18,... | collective-permute-start | bytes 147464 | tf_op jit(solution)/shard_map/ppermute | solution.py:191
  3.7 1.0 %pack.1.refs_2_ = bf16[32,3,8,128]{3,2,1,0:T(8,128)(2,1)S(1)} custom-call(s32[4,4]{1,0:T(4,128)} %pair_ref.1, s32[4,32]{1,0:T(4,128)} %at_ref.1, bf16[4,2,8,8,128]{4,3,2,1,0:T(8,128)(2,1)} %bitcast.7), custom_call_target="tpu_custom_call" | custom-call | flops 4194304 | bytes 1048576 | tf_op jit(solution)/shard_map/pack/pallas_call | solution.py:220
  4.7 0.0 collective-permute-done.refs_0_.first_ref
  4.7 3.5 %collective-permute-done.1.refs_1_.second_ref = bf16[192,128]{1,0:T(8,128)(2,1)S(1)} collective-permute-done((bf16[192,128]{1,0:T(8,128)(2,1)S(1)}, bf16[192,128]{1,0:T(8,128)(2,1)S(1)}, u32[]{:S(2)}, u32[]{:S(2)}) %collective-permute-start.1) | collective-permute-done | bytes 49184 | tf_op jit(solution)/shard_map/ppermute | solution.py:191
  8.2 0.1 halos.1
  8.3 14.0 %all_to_all.10.in_ref = bf16[32,3,8,128]{3,2,1,0:T(8,128)(2,1)S(1)} all-to-all(bf16[32,3,8,128]{3,2,1,0:T(8,128)(2,1)S(1)} %halos.1), channel_id=1, replica_groups={{92,88,84,80,76,72,68,64,124,120,116,112,108,104,100,96,28,24,20,16,12,..., dimensions={0} | all-to-all | bytes 393216 | tf_op jit(solution)/shard_map/all_to_all | solution.py:198
  22.3 0.0 copy-done
  22.3 1.3 %select.1 = (bf16[32,12,8,128]{3,2,1,0:T(8,128)(2,1)S(1)}, f32[8,3,8,8,128]{4,3,2,1,0:T(8,128)S(1)}) custom-call(bf16[32,3,8,128]{3,2,1,0:T(8,128)(2,1)S(1)} %all_to_all.10.in_ref, bf16[8,2,8,8,128]{4,3,2,1,0:T(8,128)(2,1)S(1)} %bitcast.5, bf16[192,128]{1,0:T(8,128)(2,1)S(1)} %collective-permute-done.refs_0_.first_ref, ...), custom_call_target="tpu_custom_call" | custom-call | tf_op jit(solution)/shard_map/select/pallas_call | solution.py:239
  23.7 15.2 %all_to_all.11.source_ref = bf16[32,12,8,128]{3,2,1,0:T(8,128)(2,1)S(1)} all-to-all(bf16[32,12,8,128]{3,2,1,0:T(8,128)(2,1)S(1)} %get-tuple-element.11), channel_id=1, replica_groups={{88,92,80,84,72,76,64,68,120,124,112,116,104,108,96,100,24,28,16,20,8,1..., dimensions={0} | all-to-all | bytes 1572864 | tf_op jit(solution)/shard_map/all_to_all | solution.py:198
  38.8 2.5 %correlate.1 = bf16[4,4,2,2,9,8,128]{6,5,4,3,2,1,0:T(8,128)(2,1)} custom-call(bf16[32,12,8,128]{3,2,1,0:T(8,128)(2,1)S(1)} %all_to_all.11.source_ref, f32[8,3,8,8,128]{4,3,2,1,0:T(8,128)S(1)} %get-tuple-element.12.green_ref), custom_call_target="tpu_custom_call" | custom-call | tf_op jit(solution)/shard_map/correlate/pallas_call | solution.py:258
Async XLA Ops:
  0.0 22.3 %copy-start = (bf16[4,2,2,8,8,128]{5,4,3,2,1,0:T(8,128)(2,1)S(1)}, bf16[4,2,2,8,8,128]{5,4,3,2,1,0:T(8,128)(2,1)}, u32[]{:S(2)}) copy-start(bf16[4,2,2,8,8,128]{5,4,3,2,1,0:T(8,128)(2,1)} %param.5) | copy-start | bytes 786436
  1.2 3.5 %collective-permute-start = (bf16[192,128]{1,0:T(8,128)(2,1)S(1)}, bf16[192,128]{1,0:T(8,128)(2,1)S(1)}, u32[]{:S(2)}, u32[]{:S(2)}) collective-permute-start(bf16[192,128]{1,0:T(8,128)(2,1)S(1)} %get-tuple-element.9), channel_id=1, source_target_pairs={{0,1},{1,0},{2,3},{3,2},{4,5},{5,4},{6,7},{7,6},{8,9},{9,8},{10,11... | collective-permute-start | bytes 147464 | tf_op jit(solution)/shard_map/ppermute | solution.py:192
  1.3 6.9 %collective-permute-start.1 = (bf16[192,128]{1,0:T(8,128)(2,1)S(1)}, bf16[192,128]{1,0:T(8,128)(2,1)S(1)}, u32[]{:S(2)}, u32[]{:S(2)}) collective-permute-start(bf16[192,128]{1,0:T(8,128)(2,1)S(1)} %get-tuple-element.10), channel_id=1, source_target_pairs={{1,2},{2,1},{5,6},{6,5},{9,10},{10,9},{13,14},{14,13},{17,18},{18,... | collective-permute-start | bytes 147464 | tf_op jit(solution)/shard_map/ppermute | solution.py:191
